TPU v7x, 512 devices: a whole 4x8x8 slice. The times are simulated.
512 devices in a mesh: tm: 16 (over y_lo, x, core), sx: 8 (over z), sy: 4 (over y_hi).
Axes of the slice: x: 4, y: 8 (y_hi: 4, y_lo: 2; y = y_hi * 2 + y_lo), z: 8, core: 2. Of those that a mesh axis runs over, the one named last changes fastest.
Arguments:
- initial: float32 [2048, 2048], P('sx', 'sy'), may hold values from 0.5 to 1.5
- kappa: float32 [2048, 2048], P('sx', 'sy'), may hold values from 0.0016 to 0.016
- c_guess: float32 [16, 2048, 2048], P('tm', 'sx', 'sy'), may hold values from 0.5 to 1.5
Outputs:
- c_values: float32 [16, 2048, 2048], P('tm', 'sx', 'sy')
- f_values: float32 [16, 2048, 2048], P('tm', 'sx', 'sy')
All inputs are finite; a program needn't handle non-finite values.
Results may differ from a plain program's by a relative error of at most 0.00002.
Values sent between devices are 32-bit elements; how exact they have to be, the bound alone decides.
A program may use at most 64 MiB of HBM per device.

v0:
```python
import jax
import jax.numpy as jnp
from jax import lax
from jax.sharding import PartitionSpec as P


def with_halo(x, sides, width):
    for axis, dim in sides:
        size, length = (lax.axis_size(axis), x.shape[dim])
        up = [(i, (i + 1) % size) for i in range(size - 1)]
        down = [(j, i) for i, j in up]
        last = lax.slice_in_dim(x, length - width, length, axis=dim)
        leading = lax.slice_in_dim(x, 0, width, axis=dim)
        before = lax.ppermute(last, axis, up)
        after = lax.ppermute(leading, axis, down)
        x = jnp.concatenate([before, x, after], axis=dim)
    return x


def shifted(x, axis, by):
    length = lax.axis_size(axis)
    pairs = [(i, i + by) for i in range(length) if 0 <= i + by < length]
    return lax.ppermute(x, axis, pairs)


def on_device(initial, kappa, c_guess):
    index = lax.axis_index("tm")
    count = lax.axis_size("tm")
    first = index == 0
    is_odd = index % 2 == 1

    def spread(field):
        flux = kappa * field * field
        padded = with_halo(flux, (("sx", 0), ("sy", 1)), 1)
        return (
            padded[2:, 1:-1] + padded[:-2, 1:-1] + padded[1:-1, 2:] + padded[1:-1, :-2] - 4.0 * flux
        )

    def earlier(stack, keep):
        moved = shifted(stack, "tm", 1)
        head = moved[0]
        if keep:
            head = jnp.where(first, initial, head)
        head_lap = spread(head)
        others = moved[1:]
        return (head, head_lap, others)

    guess = c_guess[0]
    prev_w, lap_w, unused = earlier(guess[None], True)
    fine = prev_w + lap_w
    lap_f = spread(fine)
    value = fine + lap_f
    first_rhs = value - prev_w - 2.0 * lap_w
    quarter = prev_w + 4.0 * lap_w
    value_prev, lap_v, others = earlier(jnp.stack([value, quarter]), False)
    second_rhs = jnp.where(is_odd, value_prev + 2.0 * lap_v + first_rhs - others[0], 0.0)
    level = initial
    for turn in range(count):
        behind = shifted(level, "tm", 1)
        stepped = behind + 4.0 * spread(behind) + second_rhs
        level = jnp.where(first, initial, jnp.where(is_odd, stepped, behind))
    even_lap = spread(level)
    new_c = jnp.where(is_odd, level, level + 2.0 * even_lap + first_rhs)
    prev_n, lap_n, unused = earlier(new_c[None], True)
    f_out = prev_n + lap_n
    return (new_c[None], f_out[None])


def solution(mesh):
    return jax.shard_map(
        on_device,
        mesh=mesh,
        in_specs=(P("sx", "sy"), P("sx", "sy"), P("tm", "sx", "sy")),
        out_specs=(P("tm", "sx", "sy"), P("tm", "sx", "sy")),
        check_vma=False,
    )
```

profile of v0, /device:TPU:56, one launch (start us, length us, event | category | flops | bytes accessed | tf_op | source)
XLA Modules:
  0.0 676.8 jit_solution(10769111629865102710)
XLA Ops:
  2.6 10.9 %collective-permute-done.5 = f32[1,256,512]{2,1,0:T(8,128)S(1)} collective-permute-done((f32[1,256,512]{2,1,0:T(8,128)}, f32[1,256,512]{2,1,0:T(8,128)S(1)}, u32[]{:S(2)}, u32[]{:S(2)}) %collective-permute-start.5) | collective-permute-done | bytes 524320 | tf_op jit(solution)/shard_map/ppermute | solution.py:23
  31.6 5.3 collective-permute-done.9
  42.9 5.7 collective-permute-done.10
  55.7 5.3 collective-permute-done.13
  65.8 20.0 %collective-permute-done = f32[256,512]{1,0:T(8,128)S(1)} collective-permute-done((f32[256,512]{1,0:T(8,128)S(1)}, f32[256,512]{1,0:T(8,128)S(1)}, u32[]{:S(2)}, u32[]{:S(2)}) %collective-permute-start) | collective-permute-done | bytes 524320 | tf_op jit(solution)/shard_map/ppermute | solution.py:23
  104.3 6.1 collective-permute-start.3
  112.7 5.9 collective-permute-done.4
  118.6 5.4 fusion.174
  125.9 10.7 %collective-permute-done.19 = f32[256,512]{1,0:T(8,128)S(1)} collective-permute-done((f32[256,512]{1,0:T(8,128)S(1)}, f32[256,512]{1,0:T(8,128)S(1)}, u32[]{:S(2)}, u32[]{:S(2)}) %collective-permute-start.19) | collective-permute-done | bytes 524320 | tf_op jit(solution)/shard_map/ppermute | solution.py:23
  160.7 10.7 %collective-permute-done.24 = f32[256,512]{1,0:T(8,128)S(1)} collective-permute-done((f32[256,512]{1,0:T(8,128)S(1)}, f32[256,512]{1,0:T(8,128)S(1)}, u32[]{:S(2)}, u32[]{:S(2)}) %collective-permute-start.24) | collective-permute-done | bytes 524320 | tf_op jit(solution)/shard_map/ppermute | solution.py:23
  194.5 10.7 %collective-permute-done.29 = f32[256,512]{1,0:T(8,128)S(1)} collective-permute-done((f32[256,512]{1,0:T(8,128)S(1)}, f32[256,512]{1,0:T(8,128)S(1)}, u32[]{:S(2)}, u32[]{:S(2)}) %collective-permute-start.29) | collective-permute-done | bytes 524320 | tf_op jit(solution)/shard_map/ppermute | solution.py:23
  221.7 5.3 collective-permute-done.33
  229.3 10.7 %collective-permute-done.34 = f32[256,512]{1,0:T(8,128)S(1)} collective-permute-done((f32[256,512]{1,0:T(8,128)S(1)}, f32[256,512]{1,0:T(8,128)S(1)}, u32[]{:S(2)}, u32[]{:S(2)}) %collective-permute-start.34) | collective-permute-done | bytes 524320 | tf_op jit(solution)/shard_map/ppermute | solution.py:23
  263.0 10.7 %collective-permute-done.39 = f32[256,512]{1,0:T(8,128)S(1)} collective-permute-done((f32[256,512]{1,0:T(8,128)S(1)}, f32[256,512]{1,0:T(8,128)S(1)}, u32[]{:S(2)}, u32[]{:S(2)}) %collective-permute-start.39) | collective-permute-done | bytes 524320 | tf_op jit(solution)/shard_map/ppermute | solution.py:23
  288.2 5.3 collective-permute-done.43
  295.8 10.7 %collective-permute-done.44 = f32[256,512]{1,0:T(8,128)S(1)} collective-permute-done((f32[256,512]{1,0:T(8,128)S(1)}, f32[256,512]{1,0:T(8,128)S(1)}, u32[]{:S(2)}, u32[]{:S(2)}) %collective-permute-start.44) | collective-permute-done | bytes 524320 | tf_op jit(solution)/shard_map/ppermute | solution.py:23
  328.7 10.7 %collective-permute-done.49 = f32[256,512]{1,0:T(8,128)S(1)} collective-permute-done((f32[256,512]{1,0:T(8,128)S(1)}, f32[256,512]{1,0:T(8,128)S(1)}, u32[]{:S(2)}, u32[]{:S(2)}) %collective-permute-start.49) | collective-permute-done | bytes 524320 | tf_op jit(solution)/shard_map/ppermute | solution.py:23
  353.9 5.3 collective-permute-done.53
  361.5 10.7 %collective-permute-done.54 = f32[256,512]{1,0:T(8,128)S(1)} collective-permute-done((f32[256,512]{1,0:T(8,128)S(1)}, f32[256,512]{1,0:T(8,128)S(1)}, u32[]{:S(2)}, u32[]{:S(2)}) %collective-permute-start.54) | collective-permute-done | bytes 524320 | tf_op jit(solution)/shard_map/ppermute | solution.py:23
  394.4 10.7 %collective-permute-done.59 = f32[256,512]{1,0:T(8,128)S(1)} collective-permute-done((f32[256,512]{1,0:T(8,128)S(1)}, f32[256,512]{1,0:T(8,128)S(1)}, u32[]{:S(2)}, u32[]{:S(2)}) %collective-permute-start.59) | collective-permute-done | bytes 524320 | tf_op jit(solution)/shard_map/ppermute | solution.py:23
  419.6 5.3 collective-permute-done.63
  427.3 10.7 %collective-permute-done.64 = f32[256,512]{1,0:T(8,128)S(1)} collective-permute-done((f32[256,512]{1,0:T(8,128)S(1)}, f32[256,512]{1,0:T(8,128)S(1)}, u32[]{:S(2)}, u32[]{:S(2)}) %collective-permute-start.64) | collective-permute-done | bytes 524320 | tf_op jit(solution)/shard_map/ppermute | solution.py:23
  460.1 10.7 %collective-permute-done.69 = f32[256,512]{1,0:T(8,128)S(1)} collective-permute-done((f32[256,512]{1,0:T(8,128)S(1)}, f32[256,512]{1,0:T(8,128)S(1)}, u32[]{:S(2)}, u32[]{:S(2)}) %collective-permute-start.69) | collective-permute-done | bytes 524320 | tf_op jit(solution)/shard_map/ppermute | solution.py:23
  485.3 5.3 collective-permute-done.73
  493.0 10.7 %collective-permute-done.74 = f32[256,512]{1,0:T(8,128)S(1)} collective-permute-done((f32[256,512]{1,0:T(8,128)S(1)}, f32[256,512]{1,0:T(8,128)S(1)}, u32[]{:S(2)}, u32[]{:S(2)}) %collective-permute-start.74) | collective-permute-done | bytes 524320 | tf_op jit(solution)/shard_map/ppermute | solution.py:23
  518.2 5.3 collective-permute-done.78
  525.8 10.7 %collective-permute-done.79 = f32[256,512]{1,0:T(8,128)S(1)} collective-permute-done((f32[256,512]{1,0:T(8,128)S(1)}, f32[256,512]{1,0:T(8,128)S(1)}, u32[]{:S(2)}, u32[]{:S(2)}) %collective-permute-start.79) | collective-permute-done | bytes 524320 | tf_op jit(solution)/shard_map/ppermute | solution.py:23
  551.0 5.3 collective-permute-done.83
  558.7 10.7 %collective-permute-done.84 = f32[256,512]{1,0:T(8,128)S(1)} collective-permute-done((f32[256,512]{1,0:T(8,128)S(1)}, f32[256,512]{1,0:T(8,128)S(1)}, u32[]{:S(2)}, u32[]{:S(2)}) %collective-permute-start.84) | collective-permute-done | bytes 524320 | tf_op jit(solution)/shard_map/ppermute | solution.py:23
  591.5 10.7 %collective-permute-done.89 = f32[256,512]{1,0:T(8,128)S(1)} collective-permute-done((f32[256,512]{1,0:T(8,128)S(1)}, f32[256,512]{1,0:T(8,128)S(1)}, u32[]{:S(2)}, u32[]{:S(2)}) %collective-permute-start.89) | collective-permute-done | bytes 524320 | tf_op jit(solution)/shard_map/ppermute | solution.py:23
  616.7 5.3 collective-permute-done.93
  645.0 10.7 %collective-permute-done.98 = f32[1,256,512]{2,1,0:T(8,128)S(1)} collective-permute-done((f32[1,256,512]{2,1,0:T(8,128)S(1)}, f32[1,256,512]{2,1,0:T(8,128)S(1)}, u32[]{:S(2)}, u32[]{:S(2)}) %collective-permute-start.98) | collective-permute-done | bytes 524320 | tf_op jit(solution)/shard_map/ppermute | solution.py:23
  (280 shorter events, 396.9 us)
Async XLA Ops:
  0.6 12.8 %collective-permute-start.5 = (f32[1,256,512]{2,1,0:T(8,128)}, f32[1,256,512]{2,1,0:T(8,128)S(1)}, u32[]{:S(2)}, u32[]{:S(2)}) collective-permute-start(f32[1,256,512]{2,1,0:T(8,128)} %param.5), channel_id=1, source_target_pairs={{0,32},{32,64},{64,96},{96,128},{128,160},{160,192},{192,224},{224... | collective-permute-start | bytes 1572872 | tf_op jit(solution)/shard_map/ppermute | solution.py:23
  29.1 7.8 %collective-permute-start.9 = (f32[258,1]{1,0:T(8,128)S(1)}, f32[258,1]{1,0:T(8,128)S(1)}, u32[]{:S(2)}, u32[]{:S(2)}) collective-permute-start(f32[258,1]{1,0:T(8,128)S(1)} %get-tuple-element.47), channel_id=1, source_target_pairs={{0,1},{1,2},{2,3},{4,5},{5,6},{6,7},{8,9},{9,10},{10,11},{12,13},{... | collective-permute-start | bytes 3104 | tf_op jit(solution)/shard_map/ppermute | solution.py:14
  53.1 7.8 %collective-permute-start.13 = (f32[258,1]{1,0:T(8,128)S(1)}, f32[258,1]{1,0:T(8,128)S(1)}, u32[]{:S(2)}, u32[]{:S(2)}) collective-permute-start(f32[258,1]{1,0:T(8,128)S(1)} %get-tuple-element.45), channel_id=1, source_target_pairs={{0,1},{1,2},{2,3},{4,5},{5,6},{6,7},{8,9},{9,10},{10,11},{12,13},{... | collective-permute-start | bytes 3104 | tf_op jit(solution)/shard_map/ppermute | solution.py:14
  61.8 24.0 %collective-permute-start.14 = (f32[2,256,512]{2,1,0:T(8,128)S(1)}, f32[2,256,512]{2,1,0:T(8,128)S(1)}, u32[]{:S(2)}, u32[]{:S(2)}) collective-permute-start(f32[2,256,512]{2,1,0:T(8,128)S(1)} %pad_maximum_fusion), channel_id=1, source_target_pairs={{0,32},{32,64},{64,96},{96,128},{128,160},{160,192},{192,224},{224... | collective-permute-start | bytes 3145736 | tf_op jit(solution)/shard_map/ppermute | solution.py:23
  63.8 21.9 %collective-permute-start = (f32[256,512]{1,0:T(8,128)S(1)}, f32[256,512]{1,0:T(8,128)S(1)}, u32[]{:S(2)}, u32[]{:S(2)}) collective-permute-start(f32[256,512]{1,0:T(8,128)S(1)} %copy-done.1), channel_id=1, source_target_pairs={{0,32},{32,64},{64,96},{96,128},{128,160},{160,192},{192,224},{224... | collective-permute-start | bytes 1572872 | tf_op jit(solution)/shard_map/ppermute | solution.py:23
  85.9 12.3 %collective-permute-start.16 = (f32[1,512]{1,0:T(1,128)S(1)}, f32[1,512]{1,0:T(1,128)S(1)}, u32[]{:S(2)}, u32[]{:S(2)}) collective-permute-start(f32[1,512]{1,0:T(1,128)S(1)} %get-tuple-element.84), channel_id=1, source_target_pairs={{0,4},{4,8},{8,12},{12,16},{16,20},{20,24},{24,28},{1,5},{5,9},{9,... | collective-permute-start | bytes 6152 | tf_op jit(solution)/shard_map/ppermute | solution.py:14
  92.4 11.1 %collective-permute-start.2 = (f32[1,512]{1,0:T(1,128)S(1)}, f32[1,512]{1,0:T(1,128)S(1)}, u32[]{:S(2)}, u32[]{:S(2)}) collective-permute-start(f32[1,512]{1,0:T(1,128)S(1)} %get-tuple-element.92), channel_id=1, source_target_pairs={{0,4},{4,8},{8,12},{12,16},{16,20},{20,24},{24,28},{1,5},{5,9},{9,... | collective-permute-start | bytes 6152 | tf_op jit(solution)/shard_map/ppermute | solution.py:14
  99.1 12.7 %collective-permute-start.17 = (f32[258,1]{1,0:T(8,128)}, f32[258,1]{1,0:T(8,128)S(1)}, u32[]{:S(2)}, u32[]{:S(2)}) collective-permute-start(f32[258,1]{1,0:T(8,128)} %get-tuple-element.42), channel_id=1, source_target_pairs={{1,0},{2,1},{3,2},{5,4},{6,5},{7,6},{9,8},{10,9},{11,10},{13,12},{... | collective-permute-start | bytes 3104 | tf_op jit(solution)/shard_map/ppermute | solution.py:15
  102.2 9.6 %collective-permute-start.18 = (f32[258,1]{1,0:T(8,128)}, f32[258,1]{1,0:T(8,128)}, u32[]{:S(2)}, u32[]{:S(2)}) collective-permute-start(f32[258,1]{1,0:T(8,128)} %get-tuple-element.43), channel_id=1, source_target_pairs={{0,1},{1,2},{2,3},{4,5},{5,6},{6,7},{8,9},{9,10},{10,11},{12,13},{... | collective-permute-start | bytes 3104 | tf_op jit(solution)/shard_map/ppermute | solution.py:14
  104.3 8.3 %collective-permute-start.3 = (f32[258,1]{1,0:T(8,128)}, f32[258,1]{1,0:T(8,128)}, u32[]{:S(2)}, u32[]{:S(2)}) collective-permute-start(f32[258,1]{1,0:T(8,128)} %get-tuple-element.48), channel_id=1, source_target_pairs={{1,0},{2,1},{3,2},{5,4},{6,5},{7,6},{9,8},{10,9},{11,10},{13,12},{... | collective-permute-start | bytes 3104 | tf_op jit(solution)/shard_map/ppermute | solution.py:15
  110.5 8.1 %collective-permute-start.4 = (f32[258,1]{1,0:T(8,128)}, f32[258,1]{1,0:T(8,128)}, u32[]{:S(2)}, u32[]{:S(2)}) collective-permute-start(f32[258,1]{1,0:T(8,128)} %get-tuple-element.49), channel_id=1, source_target_pairs={{0,1},{1,2},{2,3},{4,5},{5,6},{6,7},{8,9},{9,10},{10,11},{12,13},{... | collective-permute-start | bytes 3104 | tf_op jit(solution)/shard_map/ppermute | solution.py:14
  123.9 12.6 %collective-permute-start.19 = (f32[256,512]{1,0:T(8,128)S(1)}, f32[256,512]{1,0:T(8,128)S(1)}, u32[]{:S(2)}, u32[]{:S(2)}) collective-permute-start(f32[256,512]{1,0:T(8,128)S(1)} %get-tuple-element.4), channel_id=1, source_target_pairs={{0,32},{32,64},{64,96},{96,128},{128,160},{160,192},{192,224},{224... | collective-permute-start | bytes 1572872 | tf_op jit(solution)/shard_map/ppermute | solution.py:23
  158.8 12.6 %collective-permute-start.24 = (f32[256,512]{1,0:T(8,128)S(1)}, f32[256,512]{1,0:T(8,128)S(1)}, u32[]{:S(2)}, u32[]{:S(2)}) collective-permute-start(f32[256,512]{1,0:T(8,128)S(1)} %fusion.147), channel_id=1, source_target_pairs={{0,32},{32,64},{64,96},{96,128},{128,160},{160,192},{192,224},{224... | collective-permute-start | bytes 1572872 | tf_op jit(solution)/shard_map/ppermute | solution.py:23
  192.6 12.6 %collective-permute-start.29 = (f32[256,512]{1,0:T(8,128)S(1)}, f32[256,512]{1,0:T(8,128)S(1)}, u32[]{:S(2)}, u32[]{:S(2)}) collective-permute-start(f32[256,512]{1,0:T(8,128)S(1)} %fusion.138), channel_id=1, source_target_pairs={{0,32},{32,64},{64,96},{96,128},{128,160},{160,192},{192,224},{224... | collective-permute-start | bytes 1572872 | tf_op jit(solution)/shard_map/ppermute | solution.py:23
  219.1 7.8 %collective-permute-start.33 = (f32[258,1]{1,0:T(8,128)S(1)}, f32[258,1]{1,0:T(8,128)S(1)}, u32[]{:S(2)}, u32[]{:S(2)}) collective-permute-start(f32[258,1]{1,0:T(8,128)S(1)} %get-tuple-element.37), channel_id=1, source_target_pairs={{0,1},{1,2},{2,3},{4,5},{5,6},{6,7},{8,9},{9,10},{10,11},{12,13},{... | collective-permute-start | bytes 3104 | tf_op jit(solution)/shard_map/ppermute | solution.py:14
  227.4 12.6 %collective-permute-start.34 = (f32[256,512]{1,0:T(8,128)S(1)}, f32[256,512]{1,0:T(8,128)S(1)}, u32[]{:S(2)}, u32[]{:S(2)}) collective-permute-start(f32[256,512]{1,0:T(8,128)S(1)} %fusion.129), channel_id=1, source_target_pairs={{0,32},{32,64},{64,96},{96,128},{128,160},{160,192},{192,224},{224... | collective-permute-start | bytes 1572872 | tf_op jit(solution)/shard_map/ppermute | solution.py:23
  261.1 12.6 %collective-permute-start.39 = (f32[256,512]{1,0:T(8,128)S(1)}, f32[256,512]{1,0:T(8,128)S(1)}, u32[]{:S(2)}, u32[]{:S(2)}) collective-permute-start(f32[256,512]{1,0:T(8,128)S(1)} %fusion.120), channel_id=1, source_target_pairs={{0,32},{32,64},{64,96},{96,128},{128,160},{160,192},{192,224},{224... | collective-permute-start | bytes 1572872 | tf_op jit(solution)/shard_map/ppermute | solution.py:23
  285.6 7.8 %collective-permute-start.43 = (f32[258,1]{1,0:T(8,128)S(1)}, f32[258,1]{1,0:T(8,128)S(1)}, u32[]{:S(2)}, u32[]{:S(2)}) collective-permute-start(f32[258,1]{1,0:T(8,128)S(1)} %get-tuple-element.33), channel_id=1, source_target_pairs={{0,1},{1,2},{2,3},{4,5},{5,6},{6,7},{8,9},{9,10},{10,11},{12,13},{... | collective-permute-start | bytes 3104 | tf_op jit(solution)/shard_map/ppermute | solution.py:14
  293.9 12.6 %collective-permute-start.44 = (f32[256,512]{1,0:T(8,128)S(1)}, f32[256,512]{1,0:T(8,128)S(1)}, u32[]{:S(2)}, u32[]{:S(2)}) collective-permute-start(f32[256,512]{1,0:T(8,128)S(1)} %fusion.111), channel_id=1, source_target_pairs={{0,32},{32,64},{64,96},{96,128},{128,160},{160,192},{192,224},{224... | collective-permute-start | bytes 1572872 | tf_op jit(solution)/shard_map/ppermute | solution.py:23
  326.8 12.6 %collective-permute-start.49 = (f32[256,512]{1,0:T(8,128)S(1)}, f32[256,512]{1,0:T(8,128)S(1)}, u32[]{:S(2)}, u32[]{:S(2)}) collective-permute-start(f32[256,512]{1,0:T(8,128)S(1)} %fusion.102), channel_id=1, source_target_pairs={{0,32},{32,64},{64,96},{96,128},{128,160},{160,192},{192,224},{224... | collective-permute-start | bytes 1572872 | tf_op jit(solution)/shard_map/ppermute | solution.py:23
  351.4 7.8 %collective-permute-start.53 = (f32[258,1]{1,0:T(8,128)S(1)}, f32[258,1]{1,0:T(8,128)S(1)}, u32[]{:S(2)}, u32[]{:S(2)}) collective-permute-start(f32[258,1]{1,0:T(8,128)S(1)} %get-tuple-element.29), channel_id=1, source_target_pairs={{0,1},{1,2},{2,3},{4,5},{5,6},{6,7},{8,9},{9,10},{10,11},{12,13},{... | collective-permute-start | bytes 3104 | tf_op jit(solution)/shard_map/ppermute | solution.py:14
  359.6 12.6 %collective-permute-start.54 = (f32[256,512]{1,0:T(8,128)S(1)}, f32[256,512]{1,0:T(8,128)S(1)}, u32[]{:S(2)}, u32[]{:S(2)}) collective-permute-start(f32[256,512]{1,0:T(8,128)S(1)} %fusion.93), channel_id=1, source_target_pairs={{0,32},{32,64},{64,96},{96,128},{128,160},{160,192},{192,224},{224... | collective-permute-start | bytes 1572872 | tf_op jit(solution)/shard_map/ppermute | solution.py:23
  392.5 12.6 %collective-permute-start.59 = (f32[256,512]{1,0:T(8,128)S(1)}, f32[256,512]{1,0:T(8,128)S(1)}, u32[]{:S(2)}, u32[]{:S(2)}) collective-permute-start(f32[256,512]{1,0:T(8,128)S(1)} %fusion.84), channel_id=1, source_target_pairs={{0,32},{32,64},{64,96},{96,128},{128,160},{160,192},{192,224},{224... | collective-permute-start | bytes 1572872 | tf_op jit(solution)/shard_map/ppermute | solution.py:23
  417.1 7.8 %collective-permute-start.63 = (f32[258,1]{1,0:T(8,128)S(1)}, f32[258,1]{1,0:T(8,128)S(1)}, u32[]{:S(2)}, u32[]{:S(2)}) collective-permute-start(f32[258,1]{1,0:T(8,128)S(1)} %get-tuple-element.25), channel_id=1, source_target_pairs={{0,1},{1,2},{2,3},{4,5},{5,6},{6,7},{8,9},{9,10},{10,11},{12,13},{... | collective-permute-start | bytes 3104 | tf_op jit(solution)/shard_map/ppermute | solution.py:14
  425.3 12.6 %collective-permute-start.64 = (f32[256,512]{1,0:T(8,128)S(1)}, f32[256,512]{1,0:T(8,128)S(1)}, u32[]{:S(2)}, u32[]{:S(2)}) collective-permute-start(f32[256,512]{1,0:T(8,128)S(1)} %fusion.75), channel_id=1, source_target_pairs={{0,32},{32,64},{64,96},{96,128},{128,160},{160,192},{192,224},{224... | collective-permute-start | bytes 1572872 | tf_op jit(solution)/shard_map/ppermute | solution.py:23
  458.2 12.6 %collective-permute-start.69 = (f32[256,512]{1,0:T(8,128)S(1)}, f32[256,512]{1,0:T(8,128)S(1)}, u32[]{:S(2)}, u32[]{:S(2)}) collective-permute-start(f32[256,512]{1,0:T(8,128)S(1)} %fusion.66), channel_id=1, source_target_pairs={{0,32},{32,64},{64,96},{96,128},{128,160},{160,192},{192,224},{224... | collective-permute-start | bytes 1572872 | tf_op jit(solution)/shard_map/ppermute | solution.py:23
  491.0 12.6 %collective-permute-start.74 = (f32[256,512]{1,0:T(8,128)S(1)}, f32[256,512]{1,0:T(8,128)S(1)}, u32[]{:S(2)}, u32[]{:S(2)}) collective-permute-start(f32[256,512]{1,0:T(8,128)S(1)} %fusion.57), channel_id=1, source_target_pairs={{0,32},{32,64},{64,96},{96,128},{128,160},{160,192},{192,224},{224... | collective-permute-start | bytes 1572872 | tf_op jit(solution)/shard_map/ppermute | solution.py:23
  523.9 12.6 %collective-permute-start.79 = (f32[256,512]{1,0:T(8,128)S(1)}, f32[256,512]{1,0:T(8,128)S(1)}, u32[]{:S(2)}, u32[]{:S(2)}) collective-permute-start(f32[256,512]{1,0:T(8,128)S(1)} %fusion.48), channel_id=1, source_target_pairs={{0,32},{32,64},{64,96},{96,128},{128,160},{160,192},{192,224},{224... | collective-permute-start | bytes 1572872 | tf_op jit(solution)/shard_map/ppermute | solution.py:23
  556.7 12.6 %collective-permute-start.84 = (f32[256,512]{1,0:T(8,128)S(1)}, f32[256,512]{1,0:T(8,128)S(1)}, u32[]{:S(2)}, u32[]{:S(2)}) collective-permute-start(f32[256,512]{1,0:T(8,128)S(1)} %fusion.39), channel_id=1, source_target_pairs={{0,32},{32,64},{64,96},{96,128},{128,160},{160,192},{192,224},{224... | collective-permute-start | bytes 1572872 | tf_op jit(solution)/shard_map/ppermute | solution.py:23
  589.6 12.6 %collective-permute-start.89 = (f32[256,512]{1,0:T(8,128)S(1)}, f32[256,512]{1,0:T(8,128)S(1)}, u32[]{:S(2)}, u32[]{:S(2)}) collective-permute-start(f32[256,512]{1,0:T(8,128)S(1)} %fusion.30), channel_id=1, source_target_pairs={{0,32},{32,64},{64,96},{96,128},{128,160},{160,192},{192,224},{224... | collective-permute-start | bytes 1572872 | tf_op jit(solution)/shard_map/ppermute | solution.py:23
  614.2 7.8 %collective-permute-start.93 = (f32[258,1]{1,0:T(8,128)S(1)}, f32[258,1]{1,0:T(8,128)S(1)}, u32[]{:S(2)}, u32[]{:S(2)}) collective-permute-start(f32[258,1]{1,0:T(8,128)S(1)} %get-tuple-element.13), channel_id=1, source_target_pairs={{0,1},{1,2},{2,3},{4,5},{5,6},{6,7},{8,9},{9,10},{10,11},{12,13},{... | collective-permute-start | bytes 3104 | tf_op jit(solution)/shard_map/ppermute | solution.py:14
  643.1 12.6 %collective-permute-start.98 = (f32[1,256,512]{2,1,0:T(8,128)S(1)}, f32[1,256,512]{2,1,0:T(8,128)S(1)}, u32[]{:S(2)}, u32[]{:S(2)}) collective-permute-start(f32[1,256,512]{2,1,0:T(8,128)S(1)} %fusion.12), channel_id=1, source_target_pairs={{0,32},{32,64},{64,96},{96,128},{128,160},{160,192},{192,224},{224... | collective-permute-start | bytes 1572872 | tf_op jit(solution)/shard_map/ppermute | solution.py:23
  (83 other events, 553.1 us)
where the time goes:
time: 682 us; the launch traced here: 677 us
  waiting for transfers between devices  413 us (61%)
  starting transfers between devices  239 us (35%)
  other arithmetic  22.3 us (3%)
    ppermute x19, waiting for transfers between devices, shifted(): return lax.ppermute(x, axis, pairs)  202 us
    ppermute x42, waiting for transfers between devices, with_halo(): before = lax.ppermute(last, axis, up)  106 us
    ppermute x42, waiting for transfers between devices, with_halo(): after = lax.ppermute(leading, axis, down)  105 us
    ppermute x42, starting transfers between devices, with_halo(): before = lax.ppermute(last, axis, up)  104 us
    ppermute x42, starting transfers between devices, with_halo(): after = lax.ppermute(leading, axis, down)  98.8 us
    ppermute x19, starting transfers between devices, shifted(): return lax.ppermute(x, axis, pairs)  36.6 us
  transfers between devices with their start and end apart: 103, of which 77 were waited for; matrix products, arithmetic and copies ran while one was open for 0% of the time, Pallas kernels for 0%

commit v1 on v0

v1 whole, which is shorter than its diff:
```python
import jax
import jax.numpy as jnp
from jax import lax
from jax.experimental import pallas as pl
from jax.experimental.pallas import tpu as pltpu
from jax.sharding import PartitionSpec as P

MESH = pl.DeviceIdType.MESH
F32 = jnp.float32
ROWS, COLS = 256, 512
EXT, WIDE = ROWS + 32, COLS + 128
CHIPS = 8
WIN = 64
BLOCK = 48


def lap(v, kap):
    a = kap * v * v
    r, w = a.shape
    around = pltpu.roll(a, 1, 0) + pltpu.roll(a, r - 1, 0) + pltpu.roll(a, 1, 1) + pltpu.roll(a, w - 1, 1)
    return around - 4.0 * a


def first_part(p, kap):
    lap_p = lap(p, kap)
    f = p + lap_p
    v = f + lap(f, kap)
    return v - p - 2.0 * lap_p


def second_part(p, kap):
    lap_p = lap(p, kap)
    f = p + lap_p
    v = f + lap(f, kap)
    return v + 2.0 * lap(v, kap) - (p + 4.0 * lap_p)


def pack(x, back):
    x = x.reshape(4, 8, 8, 128)
    lane = lax.broadcasted_iota(jnp.int32, (4, 8, 128), 2)
    out = jnp.zeros((4, 8, 128), F32)
    for b in range(8):
        shift = (16 * b + back) % 128
        part = pltpu.roll(x[:, b], shift, 2) if shift else x[:, b]
        out = jnp.where((lane >= 16 * b) & (lane < 16 * b + 16), part, out)
    return out.reshape(32, 128)


def unpack(right, left):
    right, left = right.reshape(4, 8, 128), left.reshape(4, 8, 128)
    lane = lax.broadcasted_iota(jnp.int32, (4, 8, 128), 2)
    parts = []
    for b in range(8):
        r = pltpu.roll(right, (128 - 16 * b) % 128, 2) if b else right
        s = (112 - 16 * b) % 128
        l = pltpu.roll(left, s, 2) if s else left
        parts.append(jnp.where(lane < 16, r, jnp.where(lane >= 112, l, 0.0)))
    return jnp.stack(parts, axis=1).reshape(ROWS, 128)


def kernel(
    init_hbm, kap_hbm, guess_hbm, c_out, f_out,
    ie, ke, ce, strips, strips_in, got, us, ur, xs, xb, sh, eb, ga, gb,
    ld, st_s, st_r, row_s, row_r, a_s, a_r, h_s, h_r, e_s, e_r, own, sh_s, sh_r, shf_s, shf_r, eb_s, eb_r,
    u_s, u_r, x_s, x_r, xe_s, xe_r, xl, xf_s, xf_r,
):
    t, sx, sy = lax.axis_index("tm"), lax.axis_index("sx"), lax.axis_index("sy")
    nx, ny = lax.axis_size("sx"), lax.axis_size("sy")
    c, p = t // 2, lax.rem(t, 2)
    even, odd = p == 0, p == 1
    up, down = lax.rem(sx + nx - 1, nx), lax.rem(sx + 1, nx)
    left, right = lax.rem(sy + ny - 1, ny), lax.rem(sy + 1, ny)
    partner = t + 1 - 2 * p
    fields = (ie, ke, ce)

    loads = [
        pltpu.make_async_copy(src, dst.at[16 : 16 + ROWS, 0:COLS], ld.at[n])
        for n, (src, dst) in enumerate(((init_hbm, ie), (kap_hbm, ke), (guess_hbm.at[0], ce)))
    ]
    for cp in loads:
        cp.start()
    got[...] = jnp.zeros(got.shape, F32)

    barrier = pltpu.get_barrier_semaphore()

    def greet(d, carry):
        pl.semaphore_signal(barrier, inc=1, device_id={"tm": 2 * lax.rem(c + d, CHIPS) + p}, device_id_type=MESH)
        return carry

    lax.fori_loop(1, CHIPS, greet, 0)
    for there in ({"tm": partner}, {"sx": up}, {"sx": down}, {"sy": left}, {"sy": right}):
        pl.semaphore_signal(barrier, inc=1, device_id=there, device_id_type=MESH)
    pl.semaphore_wait(barrier, CHIPS - 1 + 5)

    def remote(src, dst, s, r, there):
        return pltpu.make_async_remote_copy(src, dst, s, r, device_id=there, device_id_type=MESH)

    def main_copy(i, slot):
        start = jnp.clip(32 * i - 8, 0, ROWS - BLOCK)
        src = ce.at[pl.ds(pl.multiple_of(start + 16, 8), BLOCK), 0:COLS]
        dst = got.at[slot, pl.ds(pl.multiple_of(start + 16 - 32 * i, 8), BLOCK), 0:COLS]
        return remote(src, dst, a_s.at[i], a_r.at[slot], {"tm": 2 * i + p})

    def side_copy(i, slot):
        start = jnp.clip(32 * i - 8, 0, ROWS - BLOCK)
        src = ce.at[pl.ds(pl.multiple_of(start + 16, 8), BLOCK), COLS:WIDE]
        dst = got.at[slot, pl.ds(pl.multiple_of(start + 16 - 32 * i, 8), BLOCK), COLS:WIDE]
        return remote(src, dst, h_s.at[i], h_r.at[slot], {"tm": 2 * i + p})

    def top_copy(slot):
        return remote(ce.at[0:16], got.at[slot, 0:16], e_s.at[0], e_r.at[slot], {"tm": p})

    def bottom_copy(slot):
        return remote(ce.at[EXT - 16 : EXT], got.at[slot, 48:64], e_s.at[1], e_r.at[slot], {"tm": 2 * CHIPS - 2 + p})

    loads[2].wait()
    sends_guess = t <= 12

    @pl.when(sends_guess)
    def _():
        def send(d, carry):
            main_copy(lax.rem(c + d, CHIPS), c).start()
            return carry

        lax.fori_loop(1, CHIPS, send, 0)

    loads[0].wait()
    loads[1].wait()
    for n, ref in enumerate(fields):
        strips[0, 32 * n : 32 * n + 32] = pack(ref[16 : 16 + ROWS, 0:128], 0)
        strips[1, 32 * n : 32 * n + 32] = pack(ref[16 : 16 + ROWS, COLS - 128 : COLS], 16)
    side = [
        remote(strips.at[0], strips_in.at[0], st_s.at[0], st_r.at[0], {"sy": left}),
        remote(strips.at[1], strips_in.at[1], st_s.at[1], st_r.at[1], {"sy": right}),
    ]
    for cp in side:
        cp.start()
    for cp in side:
        cp.wait_recv()
    keep_right = jnp.where(sy == ny - 1, 0.0, 1.0).astype(F32)
    keep_left = jnp.where(sy == 0, 0.0, 1.0).astype(F32)
    for n, ref in enumerate(fields):
        r, l = strips_in[0, 32 * n : 32 * n + 32], strips_in[1, 32 * n : 32 * n + 32]
        if n == 1:
            r, l = r * keep_right, l * keep_left
        ref[16 : 16 + ROWS, COLS:WIDE] = unpack(r, l)

    rows = []
    for n, ref in enumerate(fields):
        rows.append(remote(ref.at[16:32], ref.at[EXT - 16 : EXT], row_s.at[2 * n], row_r.at[2 * n], {"sx": up}))
        rows.append(remote(ref.at[EXT - 32 : EXT - 16], ref.at[0:16], row_s.at[2 * n + 1], row_r.at[2 * n + 1], {"sx": down}))
    for cp in rows:
        cp.start()

    @pl.when(sends_guess)
    def _():
        def send(d, carry):
            side_copy(lax.rem(c + d, CHIPS), c).start()
            return carry

        lax.fori_loop(1, CHIPS, send, 0)

    for cp in rows:
        cp.wait_recv()

    @pl.when(sends_guess & (c != 0))
    def _():
        top_copy(c).start()

    @pl.when(sends_guess & (c != CHIPS - 1))
    def _():
        bottom_copy(c).start()

    @pl.when(sx == 0)
    def _():
        ke[0:16] = jnp.zeros((16, WIDE), F32)

    @pl.when(sx == nx - 1)
    def _():
        ke[EXT - 16 : EXT] = jnp.zeros((16, WIDE), F32)

    shift = remote(ce.at[8 : EXT - 8], sh.at[8 : EXT - 8], sh_s, sh_r, {"tm": jnp.minimum(t + 2, 2 * CHIPS - 1)})
    pass_on = remote(sh.at[8 : EXT - 8], sh.at[8 : EXT - 8], shf_s, shf_r, {"tm": partner})
    own_even = remote(ce.at[8 : EXT - 8], eb.at[8 : EXT - 8], eb_s, eb_r, {"tm": partner})
    first_sh = pltpu.make_async_copy(ie.at[8 : EXT - 8], sh.at[8 : EXT - 8], own.at[1])

    @pl.when(odd & (c < CHIPS - 1))
    def _():
        shift.start()

    @pl.when(even)
    def _():
        own_even.start()

    @pl.when(c == 0)
    def _():
        first_sh.start()

    at = pl.multiple_of(32 * c, 32)
    mine = pltpu.make_async_copy(ce.at[pl.ds(at, WIN)], got.at[c], own.at[0])

    @pl.when(sends_guess)
    def _():
        mine.start()

    def arrive(m):
        @pl.when(m == c)
        def _():
            mine.wait()

        @pl.when(m != c)
        def _():
            main_copy(c, m).wait_recv()
            side_copy(c, m).wait_recv()

            @pl.when(c == 0)
            def _():
                top_copy(m).wait_recv()

            @pl.when(c == CHIPS - 1)
            def _():
                bottom_copy(m).wait_recv()

    def u_copy(m):
        return remote(us.at[m], ur.at[m + 1], u_s.at[m], u_r.at[m], {"tm": partner})

    def x_copy(i, j):
        dst = xb.at[pl.ds(pl.multiple_of(32 * i + 16, 8), 32)]
        return remote(xs.at[j, 16:48], dst, x_s.at[j], x_r.at[i], {"tm": 2 * j})

    def x_local(j):
        dst = xb.at[pl.ds(pl.multiple_of(32 * c + 16, 8), 32)]
        return pltpu.make_async_copy(xs.at[j, 16:48], dst, xl.at[0])

    def xe_copy(top, j):
        if top:
            return remote(xs.at[j, 8:16], xb.at[8:16], xe_s.at[j], xe_r.at[0], {"tm": 2 * j})
        return remote(xs.at[j, 48:56], xb.at[EXT - 16 : EXT - 8], xe_s.at[j], xe_r.at[1], {"tm": 2 * j})

    def xe_local(top, j):
        if top:
            return pltpu.make_async_copy(xs.at[j, 8:16], xb.at[8:16], xl.at[1])
        return pltpu.make_async_copy(xs.at[j, 48:56], xb.at[EXT - 16 : EXT - 8], xl.at[1])

    @pl.when(odd)
    def _():
        def point(m, carry):
            arrive(m)
            us[m] = second_part(got[m], ke[pl.ds(at, WIN)])
            u_copy(m).start()
            return carry

        lax.fori_loop(0, 6, point, 0)

    @pl.when(even)
    def _():
        ur[0] = second_part(ie[pl.ds(at, WIN)], ke[pl.ds(at, WIN)])
        xs[0] = ie[pl.ds(at, WIN)]

        def point(j, carry):
            kap = ke[pl.ds(at, WIN)]
            arrive(j - 1)
            part = first_part(got[j - 1], kap)

            @pl.when(j > 1)
            def _():
                u_copy(jnp.maximum(j - 2, 0)).wait_recv()

            x = xs[j - 1]
            xs[j] = x + 4.0 * lap(x, kap) + (ur[j - 1] + part)

            @pl.when(j != c)
            def _():
                x_copy(c, j).start()

                @pl.when(c == 0)
                def _():
                    xe_copy(True, j).start()

                @pl.when(c == CHIPS - 1)
                def _():
                    xe_copy(False, j).start()

            @pl.when(j == c)
            def _():
                x_local(j).start()

                @pl.when(c == CHIPS - 1)
                def _():
                    xe_local(False, j).start()

            return carry

        lax.fori_loop(1, CHIPS, point, 0)

    @pl.when(c == 0)
    def _():
        first_sh.wait()

    @pl.when(odd)
    def _():
        @pl.when(c > 0)
        def _():
            shift.wait_recv()
            pass_on.start()

        own_even.wait_recv()

    @pl.when(even & (c > 0))
    def _():
        pass_on.wait_recv()

    def ahead(b, carry):
        w = pl.ds(pl.multiple_of(32 * b + 8, 8), BLOCK)
        kap = ke[w]
        ga[b] = first_part(sh[w], kap)

        @pl.when(odd)
        def _():
            g = second_part(sh[w], kap) + first_part(eb[w], kap)
            gb[b] = g[8:40, 0:COLS]

        return carry

    lax.fori_loop(0, CHIPS, ahead, 0)

    def xf_copy(lo, hi, i):
        return remote(xb.at[lo:hi], xb.at[lo:hi], xf_s.at[i], xf_r.at[i], {"tm": partner})

    spans = [(8 if i == 0 else 32 * i + 16, EXT - 8 if i == CHIPS - 1 else 32 * i + 48) for i in range(CHIPS)]
    first_x = pltpu.make_async_copy(ie.at[8 : EXT - 8], xb.at[8 : EXT - 8], own.at[1])

    @pl.when(c == 0)
    def _():
        first_x.start()
        first_x.wait()

    @pl.when(even & (c > 0))
    def _():
        for i in range(CHIPS):

            @pl.when(c == i)
            def _():
                x_local(c).wait()
                if i == CHIPS - 1:
                    xe_local(False, c).wait()

            @pl.when(c != i)
            def _():
                x_copy(i, c).wait_recv()
                if i == 0:
                    xe_copy(True, c).wait_recv()
                if i == CHIPS - 1:
                    xe_copy(False, c).wait_recv()

            xf_copy(*spans[i], i).start()

    @pl.when(odd & (c > 0))
    def _():
        for i in range(CHIPS):
            xf_copy(*spans[i], i).wait_recv()

    def finish(b, carry):
        w = pl.ds(pl.multiple_of(32 * b + 8, 8), BLOCK)
        o = pl.ds(pl.multiple_of(32 * b, 32), 32)
        kap, x = ke[w], xb[w]
        lap_x = lap(x, kap)
        mid = x + 2.0 * lap_x + ga[b]

        @pl.when(even)
        def _():
            c_out[0, o] = mid[8:40, 0:COLS]
            f_out[0, o] = (x + lap_x)[8:40, 0:COLS]

        @pl.when(odd)
        def _():
            c_out[0, o] = (x + 4.0 * lap_x)[8:40, 0:COLS] + gb[b]
            f_out[0, o] = (mid + lap(mid, kap))[8:40, 0:COLS]

        return carry

    lax.fori_loop(0, CHIPS, finish, 0)

    for cp in side + rows:
        cp.wait_send()

    @pl.when(sends_guess)
    def _():
        def sent(d, carry):
            i = lax.rem(c + d, CHIPS)
            main_copy(i, c).wait_send()
            side_copy(i, c).wait_send()
            return carry

        lax.fori_loop(1, CHIPS, sent, 0)

        @pl.when(c != 0)
        def _():
            top_copy(c).wait_send()

        @pl.when(c != CHIPS - 1)
        def _():
            bottom_copy(c).wait_send()

    @pl.when(odd)
    def _():
        @pl.when(c < CHIPS - 1)
        def _():
            shift.wait_send()

        @pl.when(c > 0)
        def _():
            pass_on.wait_send()

        def sent(m, carry):
            u_copy(m).wait_send()
            return carry

        lax.fori_loop(0, 6, sent, 0)

    @pl.when(even)
    def _():
        own_even.wait_send()

        def sent(j, carry):
            @pl.when(j != c)
            def _():
                x_copy(c, j).wait_send()

                @pl.when(c == 0)
                def _():
                    xe_copy(True, j).wait_send()

                @pl.when(c == CHIPS - 1)
                def _():
                    xe_copy(False, j).wait_send()

            return carry

        lax.fori_loop(1, CHIPS, sent, 0)

        @pl.when(c > 0)
        def _():
            for i in range(CHIPS):
                xf_copy(*spans[i], i).wait_send()


def solution(mesh):
    dma = pltpu.SemaphoreType.DMA

    def on_device(initial, kappa, guess):
        tile = jax.ShapeDtypeStruct((1, ROWS, COLS), F32)
        wide = pltpu.VMEM((EXT, WIDE), F32)
        wins = lambda n: pltpu.VMEM((n, WIN, WIDE), F32)
        return pl.pallas_call(
            kernel,
            out_shape=(tile, tile),
            in_specs=[pl.BlockSpec(memory_space=pl.ANY)] * 3,
            out_specs=(pl.BlockSpec(memory_space=pltpu.VMEM),) * 2,
            scratch_shapes=[
                wide, wide, wide,
                pltpu.VMEM((2, 96, 128), F32), pltpu.VMEM((2, 96, 128), F32),
                wins(8), wins(6), wins(7), wins(8),
                wide, wide, wide,
                pltpu.VMEM((CHIPS, BLOCK, WIDE), F32), pltpu.VMEM((CHIPS, 32, COLS), F32),
                dma((3,)), dma((2,)), dma((2,)), dma((6,)), dma((6,)),
                dma((8,)), dma((8,)), dma((8,)), dma((8,)), dma((2,)), dma((8,)), dma((2,)),
                dma, dma, dma, dma, dma, dma,
                dma((6,)), dma((6,)), dma((8,)), dma((8,)), dma((8,)), dma((2,)), dma((2,)), dma((8,)), dma((8,)),
            ],
            compiler_params=pltpu.CompilerParams(
                collective_id=0, has_side_effects=True, vmem_limit_bytes=40 * 2**20
            ),
        )(initial, kappa, guess)

    return jax.shard_map(
        on_device,
        mesh=mesh,
        in_specs=(P("sx", "sy"), P("sx", "sy"), P("tm", "sx", "sy")),
        out_specs=(P("tm", "sx", "sy"), P("tm", "sx", "sy")),
        check_vma=False,
    )
```

time: 682 us -> 61.2 us (0.09)
  the two profiles are of different devices: /device:TPU:56 before, /device:TPU:9 now
where the time goes in v1:
time: 61.2 us; the launch traced here: 61 us
  Pallas kernels  55.6 us (91%)
  local copies, waits for them, and re-layouts  4.71 us (8%)
  between operations  0.65 us (1%)
    pallas_call x1, Pallas kernels, on_device(): pl.pallas_call(kernel, out_shape=(tile, tile), in_specs=[pl.BlockSpec(mem...  55.6 us
    unnamed x8, local copies, waits for them, and re-layouts  4.71 us

profile of v1, /device:TPU:9, one launch (start us, length us, event | category | flops | bytes accessed | tf_op | source)
XLA Modules:
  0.0 61.0 jit_solution(17495552889653319698)
XLA Ops:
  0.6 0.0 copy-start
  0.6 1.0 %copy-done = f32[256,512]{1,0:T(8,128)S(1)} copy-done((f32[256,512]{1,0:T(8,128)S(1)}, f32[256,512]{1,0:T(8,128)}, u32[]{:S(2)}) %copy-start) | copy-done | bytes 524312
  1.7 0.0 copy-start.1
  1.7 1.0 %copy-done.1 = f32[256,512]{1,0:T(8,128)S(1)} copy-done((f32[256,512]{1,0:T(8,128)S(1)}, f32[256,512]{1,0:T(8,128)}, u32[]{:S(2)}) %copy-start.1) | copy-done | bytes 524312
  2.7 0.0 copy-start.2
  2.7 1.0 %copy-done.2 = f32[1,256,512]{2,1,0:T(8,128)S(1)} copy-done((f32[1,256,512]{2,1,0:T(8,128)S(1)}, f32[1,256,512]{2,1,0:T(8,128)}, u32[]{:S(2)}) %copy-start.2) | copy-done | bytes 524312
  3.8 55.6 %shard_map.50 = (f32[1,256,512]{2,1,0:T(8,128)S(1)}, f32[1,256,512]{2,1,0:T(8,128)S(1)}) custom-call(f32[256,512]{1,0:T(8,128)S(1)} %copy-done, f32[256,512]{1,0:T(8,128)S(1)} %copy-done.1, f32[1,256,512]{2,1,0:T(8,128)S(1)} %copy-done.2), custom_call_target="tpu_custom_call" | custom-call | tf_op jit(solution)/shard_map/pallas_call | solution.py:455
  59.4 0.8 %copy.7 = f32[1,256,512]{2,1,0:T(8,128)} copy(f32[1,256,512]{2,1,0:T(8,128)S(1)} %get-tuple-element.4) | data formatting | bytes 1048576
  60.2 0.8 %copy.8 = f32[1,256,512]{2,1,0:T(8,128)} copy(f32[1,256,512]{2,1,0:T(8,128)S(1)} %get-tuple-element.5) | data formatting | bytes 1048576
Async XLA Ops:
  0.6 1.0 %copy-start = (f32[256,512]{1,0:T(8,128)S(1)}, f32[256,512]{1,0:T(8,128)}, u32[]{:S(2)}) copy-start(f32[256,512]{1,0:T(8,128)} %init_hbm.1) | copy-start | bytes 1572868
  1.7 1.0 %copy-start.1 = (f32[256,512]{1,0:T(8,128)S(1)}, f32[256,512]{1,0:T(8,128)}, u32[]{:S(2)}) copy-start(f32[256,512]{1,0:T(8,128)} %kap_hbm.1) | copy-start | bytes 1572868
  2.7 1.0 %copy-start.2 = (f32[1,256,512]{2,1,0:T(8,128)S(1)}, f32[1,256,512]{2,1,0:T(8,128)}, u32[]{:S(2)}) copy-start(f32[1,256,512]{2,1,0:T(8,128)} %guess_hbm.1) | copy-start | bytes 1572868

commit v2 on v0

v2 whole, which is shorter than its diff:
```python
import jax
import jax.numpy as jnp
from jax import lax
from jax.experimental import pallas as pl
from jax.experimental.pallas import tpu as pltpu
from jax.sharding import PartitionSpec as P

MESH = pl.DeviceIdType.MESH
F32 = jnp.float32
ROWS, COLS = 256, 512
MAIN, WIDE = 4, 5
EXT = ROWS + 32
CHIPS = 8
WIN = 64
BLOCK = 48
HALF = 144
EARLY = 5


def lap(v, kap, work):
    a = kap * v * v
    rows = a.shape[1]
    work[:, 8 : 8 + rows] = a
    lane = lax.broadcasted_iota(jnp.int32, a.shape, 2)
    r, l = pltpu.roll(a, 1, 2), pltpu.roll(a, 127, 2)
    before = jnp.where(lane == 0, jnp.concatenate([r[WIDE - 1 :], r[: WIDE - 1]], axis=0), r)
    after = jnp.where(lane == 127, jnp.concatenate([l[1:], l[:1]], axis=0), l)
    return (work[:, 7 : 7 + rows] + work[:, 9 : 9 + rows]) + (before + after) - 4.0 * a


def parts(p, kap, work, second):
    lap_p = lap(p, kap, work[0])
    f = p + lap_p
    v = f + lap(f, kap, work[1])
    g1 = v - p - 2.0 * lap_p
    if not second:
        return g1
    return g1, v + 2.0 * lap(v, kap, work[2]) - (p + 4.0 * lap_p)


def pack(x, back):
    x = x.reshape(4, 8, 8, 128)
    lane = lax.broadcasted_iota(jnp.int32, (4, 8, 128), 2)
    out = jnp.zeros((4, 8, 128), F32)
    for b in range(8):
        shift = (16 * b + back) % 128
        part = pltpu.roll(x[:, b], shift, 2) if shift else x[:, b]
        out = jnp.where((lane >= 16 * b) & (lane < 16 * b + 16), part, out)
    return out


def halo_rows(right, left, b):
    lane = lax.broadcasted_iota(jnp.int32, (8, 128), 1)
    r = pltpu.roll(right, 128 - 16 * b, 1) if b else right
    back = (112 - 16 * b) % 128
    l = pltpu.roll(left, back, 1) if back else left
    return jnp.where(lane < 16, r, jnp.where(lane >= 112, l, 0.0))


def unpack(dst, tiles, groups, skip, scale=None):
    for group in range(groups):
        tile, b = (group + skip) // 8, (group + skip) % 8
        r, l = tiles(0, tile), tiles(1, tile)
        if scale is not None:
            r, l = r * scale[0], l * scale[1]
        dst[MAIN, 8 * group : 8 * group + 8] = halo_rows(r, l, b)


def kernel(
    init_hbm, kap_hbm, guess_hbm, c_out, f_out,
    ie, ke, ce, sp, si, pt, gs, got, us, ur, xs, xb, ph, phs, qh, qhs, ga, gb, oc, of, w0, w1, w2,
    ld, st_s, st_r, co_s, co_r, row_s, row_r, a_s, a_r, h_s, h_r, e_s, e_r, sh_s, sh_r, eb_s, eb_r,
    u_s, u_r, x_s, x_r, xe_s, xe_r, o_s, o_r,
):
    t, sx, sy = lax.axis_index("tm"), lax.axis_index("sx"), lax.axis_index("sy")
    nx, ny = lax.axis_size("sx"), lax.axis_size("sy")
    c, p = t // 2, lax.rem(t, 2)
    even, odd = p == 0, p == 1
    up, down = lax.rem(sx + nx - 1, nx), lax.rem(sx + 1, nx)
    left, right = lax.rem(sy + ny - 1, ny), lax.rem(sy + 1, ny)
    partner = t + 1 - 2 * p
    sends_guess = t <= 12
    work = (w0, w1, w2)

    loads = [
        [
            pltpu.make_async_copy(src.at[:, 128 * k : 128 * k + 128], dst.at[k, 16 : 16 + ROWS], ld.at[MAIN * n + k])
            for k in range(MAIN)
        ]
        for n, (src, dst) in enumerate(((init_hbm, ie), (kap_hbm, ke), (guess_hbm.at[0], ce)))
    ]
    for n in (2, 1, 0):
        for cp in loads[n]:
            cp.start()

    barrier = pltpu.get_barrier_semaphore()
    got[...] = jnp.zeros(got.shape, F32)

    def greet(d, carry):
        pl.semaphore_signal(barrier, inc=1, device_id={"tm": lax.rem(t + d, 2 * CHIPS)}, device_id_type=MESH)
        return carry

    lax.fori_loop(1, 2 * CHIPS, greet, 0)
    near = [{"sx": up}, {"sx": down}, {"sy": left}, {"sy": right}]
    near += [{"sx": v, "sy": h} for v in (up, down) for h in (left, right)]
    for there in near:
        pl.semaphore_signal(barrier, inc=1, device_id=there, device_id_type=MESH)
    for w in work:
        w[...] = jnp.zeros(w.shape, F32)

    def remote(src, dst, s, r, there):
        return pltpu.make_async_remote_copy(src, dst, s, r, device_id=there, device_id_type=MESH)

    def strip_copies(n, lo, hi):
        copies = []
        for side, h in enumerate((left, right)):
            k = 2 * n + side
            f = pl.ds(lo, hi - lo)
            copies.append(remote(sp.at[side, f], si.at[side, f, 1:5], st_s.at[k], st_r.at[k], {"sy": h}))
            copies.append(remote(sp.at[side, f, 3], si.at[side, f, 0], co_s.at[2 * k], co_r.at[2 * k], {"sx": down, "sy": h}))
            copies.append(remote(sp.at[side, f, 0], si.at[side, f, 5], co_s.at[2 * k + 1], co_r.at[2 * k + 1], {"sx": up, "sy": h}))
        return copies

    def row_copies(n, ref):
        a, b, m = 2 * n, 2 * n + 1, pl.ds(0, MAIN)
        return [
            remote(ref.at[m, 16:32], ref.at[m, EXT - 16 : EXT], row_s.at[a], row_r.at[a], {"sx": up}),
            remote(ref.at[m, EXT - 32 : EXT - 16], ref.at[m, 0:16], row_s.at[b], row_r.at[b], {"sx": down}),
        ]

    def main_copy(i, slot):
        start = jnp.clip(32 * i - 8, 0, ROWS - BLOCK)
        src = ce.at[:, pl.ds(pl.multiple_of(start + 16, 8), BLOCK)]
        dst = got.at[slot, :, pl.ds(pl.multiple_of(start + 16 - 32 * i, 8), BLOCK)]
        return remote(src, dst, a_s.at[i], a_r.at[slot], {"tm": 2 * i + p})

    def side_copy(i, slot):
        return remote(pt.at[i], gs.at[slot], h_s.at[i], h_r.at[slot], {"tm": 2 * i + p})

    def top_copy(slot):
        return remote(ce.at[:, 0:16], got.at[slot, :, 0:16], e_s.at[0], e_r.at[slot], {"tm": p})

    def bottom_copy(slot):
        return remote(ce.at[:, EXT - 16 : EXT], got.at[slot, :, 48:64], e_s.at[1], e_r.at[slot], {"tm": 2 * CHIPS - 2 + p})

    guess_near = strip_copies(0, 2, 3) + row_copies(2, ce)
    other_near = strip_copies(1, 0, 2) + row_copies(1, ke) + row_copies(0, ie)

    def send_main(d, carry):
        main_copy(lax.rem(c + d, CHIPS), c).start()
        return carry

    def send_side(d, carry):
        side_copy(lax.rem(c + d, CHIPS), c).start()
        return carry

    for cp in loads[2]:
        cp.wait()
    sp[0, 2] = pack(ce[0, 16 : 16 + ROWS], 0)
    sp[1, 2] = pack(ce[MAIN - 1, 16 : 16 + ROWS], 16)
    pl.semaphore_wait(barrier, 2 * CHIPS - 1 + 8)
    for cp in guess_near:
        cp.start()

    @pl.when(sends_guess)
    def _():
        lax.fori_loop(1, EARLY, send_main, 0)

    for n, ref in ((0, ie), (1, ke)):
        for cp in loads[n]:
            cp.wait()
        sp[0, n] = pack(ref[0, 16 : 16 + ROWS], 0)
        sp[1, n] = pack(ref[MAIN - 1, 16 : 16 + ROWS], 16)
    for cp in other_near:
        cp.start()

    for cp in guess_near:
        cp.wait_recv()
    lane = lax.broadcasted_iota(jnp.int32, (8, 128), 1)
    for i in range(CHIPS):
        q, late = i // 2, i % 2
        back, cut = (96, 96) if late else (32, 32)
        for side in range(2):
            a, b = si[side, 2, q + late], si[side, 2, q + late + 1]
            pt[i, side] = jnp.where(lane < cut, pltpu.roll(a, back, 1), pltpu.roll(b, back, 1))

    @pl.when(sends_guess)
    def _():
        lax.fori_loop(1, CHIPS, send_side, 0)

        @pl.when(c != 0)
        def _():
            top_copy(c).start()

        @pl.when(c != CHIPS - 1)
        def _():
            bottom_copy(c).start()

        lax.fori_loop(EARLY, CHIPS, send_main, 0)

    at = pl.multiple_of(32 * c, 32)
    got[c] = ce[:, pl.ds(at, WIN)]
    gs[c] = pt[c]

    mine = pl.multiple_of(8 + 128 * p, 8)

    def shift(h):
        to = {"tm": jnp.minimum(t + 1 + h, 2 * CHIPS - 1)}
        return [
            remote(ce.at[:, pl.ds(8 + 128 * h, HALF)], ph.at[0:MAIN], sh_s.at[2 * h], sh_r.at[0], to),
            remote(si.at[:, 2, pl.ds(2 * h, 4)], phs, sh_s.at[2 * h + 1], sh_r.at[1], to),
        ]

    @pl.when(odd & (c < CHIPS - 1))
    def _():
        for cp in shift(0) + shift(1):
            cp.start()

    own_even = [
        remote(ce.at[:, pl.ds(136, HALF)], qh.at[0:MAIN], eb_s.at[0], eb_r.at[0], {"tm": partner}),
        remote(si.at[:, 2, pl.ds(2, 4)], qhs, eb_s.at[1], eb_r.at[1], {"tm": partner}),
    ]

    @pl.when(even)
    def _():
        for cp in own_even:
            cp.start()

    for cp in other_near:
        cp.wait_recv()
    keep = (jnp.where(sy == ny - 1, 0.0, 1.0).astype(F32), jnp.where(sy == 0, 0.0, 1.0).astype(F32))
    unpack(ke, lambda side, k: si[side, 1, k], EXT // 8, 6, keep)
    unpack(ie, lambda side, k: si[side, 0, k], EXT // 8, 6)

    @pl.when(sx == 0)
    def _():
        ke[:, 0:16] = jnp.zeros((WIDE, 16, 128), F32)

    @pl.when(sx == nx - 1)
    def _():
        ke[:, EXT - 16 : EXT] = jnp.zeros((WIDE, 16, 128), F32)

    def window(m):
        @pl.when(m != c)
        def _():
            main_copy(c, m).wait_recv()
            side_copy(c, m).wait_recv()

            @pl.when(c == 0)
            def _():
                top_copy(m).wait_recv()

            @pl.when(c == CHIPS - 1)
            def _():
                bottom_copy(m).wait_recv()

        r, l = gs[m, 0], gs[m, 1]
        side = jnp.concatenate([halo_rows(r, l, b) for b in range(8)], axis=0)
        return jnp.concatenate([got[m], side[None]], axis=0)

    def u_copy(m):
        return remote(us.at[m], ur.at[m + 1], u_s.at[m], u_r.at[m], {"tm": partner})

    half = c // 4

    def x_copy(i, j):
        dst = xb.at[:, pl.ds(pl.multiple_of(8 + 32 * lax.rem(i, 4), 8), 32)]
        return remote(xs.at[j, :, 16:48], dst, x_s.at[j], x_r.at[lax.rem(i, 4)], {"tm": 2 * j + i // 4})

    beyond = ((0, 8, 0, 0), (3, 40, 1, 0), (4, 16, 0, HALF - 8), (7, 48, 1, HALF - 8))

    def xe_copy(n, j):
        _, row, core, to = beyond[n]
        return remote(xs.at[j, :, row : row + 8], xb.at[:, to : to + 8], xe_s.at[j], xe_r.at[to // 128], {"tm": 2 * j + core})

    def for_x(j, act):
        @pl.when((j != c) | (half == 1))
        def _():
            act(x_copy(c, j))

        for n, (i, _, core, _) in enumerate(beyond):

            @pl.when((c == i) & ((j != i) | (core == 1)))
            def _():
                act(xe_copy(n, j))

    @pl.when(odd)
    def _():
        def point(m, carry):
            us[m] = parts(window(m), ke[:, pl.ds(at, WIN)], work, True)[1]
            u_copy(m).start()
            return carry

        lax.fori_loop(0, 6, point, 0)

    @pl.when(even)
    def _():
        kap0 = ke[:, pl.ds(at, WIN)]
        ur[0] = parts(ie[:, pl.ds(at, WIN)], kap0, work, True)[1]
        xs[0] = ie[:, pl.ds(at, WIN)]

        def point(j, carry):
            kap = ke[:, pl.ds(at, WIN)]
            part = parts(window(j - 1), kap, work, False)

            @pl.when(j > 1)
            def _():
                u_copy(jnp.maximum(j - 2, 0)).wait_recv()

            x = xs[j - 1]
            xs[j] = x + 4.0 * lap(x, kap, w2) + (ur[j - 1] + part)
            for_x(j, lambda cp: cp.start())

            @pl.when((j == c) & (half == 0))
            def _():
                xb[:, pl.ds(pl.multiple_of(8 + 32 * lax.rem(c, 4), 8), 32)] = xs[j, :, 16:48]

            @pl.when((j == c) & (c == 4))
            def _():
                xb[:, HALF - 8 : HALF] = xs[j, :, 16:24]

            return carry

        lax.fori_loop(1, CHIPS, point, 0)

    @pl.when(c == 0)
    def _():
        ph[...] = ie[:, pl.ds(mine, HALF)]
        xb[...] = ie[:, pl.ds(mine, HALF)]

    @pl.when(even)
    def _():
        qh[0:MAIN] = ce[:, 8 : 8 + HALF]
        unpack(qh, lambda side, k: si[side, 2, k], HALF // 8, 7)

    @pl.when(odd)
    def _():
        for cp in own_even:
            cp.wait_recv()
        unpack(qh, lambda side, k: qhs[side, k], HALF // 8, 7)

    @pl.when(c > 0)
    def _():
        for cp in shift(0):
            cp.wait_recv()
        unpack(ph, lambda side, k: phs[side, k], HALF // 8, 7)

    def ahead(b, carry):
        w = pl.ds(pl.multiple_of(32 * b, 32), BLOCK)
        kap = ke[:, pl.ds(pl.multiple_of(mine + 32 * b, 8), BLOCK)]
        g1, u = parts(ph[:, w], kap, work, True)
        ga[b] = g1
        gb[b] = u + parts(qh[:, w], kap, work, False)
        return carry

    lax.fori_loop(0, 4, ahead, 0)

    @pl.when(c > 0)
    def _():
        for k in range(4):

            @pl.when(odd | (c != k))
            def _():
                x_copy(k, c).wait_recv()

        xe_copy(0, c).wait_recv()

        @pl.when(odd | (c != 4))
        def _():
            xe_copy(2, c).wait_recv()

    def out_copy(b, n):
        o = pl.ds(pl.multiple_of(128 * p + 32 * b, 32), 32)
        src, dst = ((oc, c_out), (of, f_out))[n]
        return remote(src.at[b], dst.at[0, o], o_s.at[2 * b + n], o_r.at[2 * b + n], {"tm": partner})

    def finish(b, carry):
        w = pl.ds(pl.multiple_of(32 * b, 32), BLOCK)
        o = pl.ds(pl.multiple_of(128 * p + 32 * b, 32), 32)
        kap, x = ke[:, pl.ds(pl.multiple_of(mine + 32 * b, 8), BLOCK)], xb[:, w]
        lap_x = lap(x, kap, w0)
        mid = x + 2.0 * lap_x + ga[b]
        even_f = x + lap_x
        odd_c = x + 4.0 * lap_x + gb[b]
        odd_f = mid + lap(mid, kap, w1)

        def put(to_c, to_f, c_value, f_value):
            for k in range(MAIN):
                to_c[:, 128 * k : 128 * k + 128] = c_value[k, 8:40]
                to_f[:, 128 * k : 128 * k + 128] = f_value[k, 8:40]

        @pl.when(even)
        def _():
            put(c_out.at[0, o], f_out.at[0, o], mid, even_f)
            put(oc.at[b], of.at[b], odd_c, odd_f)

        @pl.when(odd)
        def _():
            put(c_out.at[0, o], f_out.at[0, o], odd_c, odd_f)
            put(oc.at[b], of.at[b], mid, even_f)

        out_copy(b, 0).start()
        out_copy(b, 1).start()
        return carry

    lax.fori_loop(0, 4, finish, 0)

    for cp in guess_near + other_near:
        cp.wait_send()

    @pl.when(sends_guess)
    def _():
        def sent(d, carry):
            i = lax.rem(c + d, CHIPS)
            main_copy(i, c).wait_send()
            side_copy(i, c).wait_send()
            return carry

        lax.fori_loop(1, CHIPS, sent, 0)

        @pl.when(c != 0)
        def _():
            top_copy(c).wait_send()

        @pl.when(c != CHIPS - 1)
        def _():
            bottom_copy(c).wait_send()

    @pl.when(odd)
    def _():
        @pl.when(c < CHIPS - 1)
        def _():
            for cp in shift(0) + shift(1):
                cp.wait_send()

        def sent(m, carry):
            u_copy(m).wait_send()
            return carry

        lax.fori_loop(0, 6, sent, 0)

    @pl.when(even)
    def _():
        for cp in own_even:
            cp.wait_send()

        def sent(j, carry):
            for_x(j, lambda cp: cp.wait_send())
            return carry

        lax.fori_loop(1, CHIPS, sent, 0)

    def landed(b, carry):
        for n in range(2):
            out_copy(b, n).wait()
        return carry

    lax.fori_loop(0, 4, landed, 0)


def solution(mesh):
    def dma(*shape):
        return pltpu.SemaphoreType.DMA(shape) if shape else pltpu.SemaphoreType.DMA

    def vmem(*shape):
        return pltpu.VMEM(shape, F32)

    def on_device(initial, kappa, guess):
        tile = jax.ShapeDtypeStruct((1, ROWS, COLS), F32)
        return pl.pallas_call(
            kernel,
            out_shape=(tile, tile),
            in_specs=[pl.BlockSpec(memory_space=pltpu.HBM)] * 3,
            out_specs=(pl.BlockSpec(memory_space=pltpu.VMEM),) * 2,
            scratch_shapes=[
                vmem(WIDE, EXT, 128), vmem(WIDE, EXT, 128), vmem(MAIN, EXT, 128),
                vmem(2, 3, 4, 8, 128), vmem(2, 3, 6, 8, 128), vmem(CHIPS, 2, 8, 128), vmem(CHIPS, 2, 8, 128),
                vmem(CHIPS, MAIN, WIN, 128), vmem(6, WIDE, WIN, 128), vmem(7, WIDE, WIN, 128), vmem(8, WIDE, WIN, 128),
                vmem(WIDE, HALF, 128), vmem(WIDE, HALF, 128), vmem(2, 4, 8, 128), vmem(WIDE, HALF, 128), vmem(2, 4, 8, 128),
                vmem(4, WIDE, BLOCK, 128), vmem(4, WIDE, BLOCK, 128), vmem(4, 32, COLS), vmem(4, 32, COLS),
                vmem(WIDE, WIN + 16, 128), vmem(WIDE, WIN + 16, 128), vmem(WIDE, WIN + 16, 128),
                dma(12), dma(4), dma(4), dma(8), dma(8), dma(6), dma(6),
                dma(8), dma(8), dma(8), dma(8), dma(2), dma(8), dma(4), dma(2), dma(2), dma(2),
                dma(6), dma(6), dma(8), dma(4), dma(8), dma(2), dma(8), dma(8),
            ],
            compiler_params=pltpu.CompilerParams(
                collective_id=0, has_side_effects=True, vmem_limit_bytes=67043328
            ),
        )(initial, kappa, guess)

    return jax.shard_map(
        on_device,
        mesh=mesh,
        in_specs=(P("sx", "sy"), P("sx", "sy"), P("tm", "sx", "sy")),
        out_specs=(P("tm", "sx", "sy"), P("tm", "sx", "sy")),
        check_vma=False,
    )
```

time: 682 us -> 52.4 us (0.08)
  the two profiles are of different devices: /device:TPU:56 before, /device:TPU:25 now
where the time goes in v2:
time: 52.4 us; the launch traced here: 52.2 us
  Pallas kernels  48.8 us (93%)
  local copies, waits for them, and re-layouts  2.72 us (5%)
  between operations  0.65 us (1%)
    pallas_call x1, Pallas kernels, on_device(): pl.pallas_call(kernel, out_shape=(tile, tile), in_specs=[pl.BlockSpec(mem...  48.8 us
    unnamed x4, local copies, waits for them, and re-layouts  2.72 us

profile of v2, /device:TPU:25, one launch (start us, length us, event | category | flops | bytes accessed | tf_op | source)
XLA Modules:
  0.0 52.2 jit_solution(6888444916301235449)
XLA Ops:
  0.6 48.8 %shard_map.50 = (f32[1,256,512]{2,1,0:T(8,128)}, f32[1,256,512]{2,1,0:T(8,128)}) custom-call(f32[256,512]{1,0:T(8,128)} %init_hbm.1, f32[256,512]{1,0:T(8,128)} %kap_hbm.1, f32[1,256,512]{2,1,0:T(8,128)} %guess_hbm.1), custom_call_target="tpu_custom_call" | custom-call | tf_op jit(solution)/shard_map/pallas_call | solution.py:470
  49.5 0.0 copy-start
  49.5 1.9 %copy.7 = f32[1,256,512]{2,1,0:T(8,128)} copy(f32[1,256,512]{2,1,0:T(8,128)} %get-tuple-element.4) | data formatting | bytes 1048576
  51.4 0.0 copy-done
  51.4 0.8 %copy.8 = f32[1,256,512]{2,1,0:T(8,128)} copy(f32[1,256,512]{2,1,0:T(8,128)S(1)} %copy-done) | data formatting | bytes 1048576
Async XLA Ops:
  49.5 1.9 %copy-start = (f32[1,256,512]{2,1,0:T(8,128)S(1)}, f32[1,256,512]{2,1,0:T(8,128)}, u32[]{:S(2)}) copy-start(f32[1,256,512]{2,1,0:T(8,128)} %get-tuple-element.5) | copy-start | bytes 1572868

commit v3 on v2

--- a/solution.py
+++ b/solution.py
@@ -14,7 +14,6 @@
 WIN = 64
 BLOCK = 48
 HALF = 144
-EARLY = 5
 
 
 def lap(v, kap, work):
@@ -57,27 +56,26 @@
     return jnp.where(lane < 16, r, jnp.where(lane >= 112, l, 0.0))
 
 
-def unpack(dst, tiles, groups, skip, scale=None):
+def unpack(dst, tiles, groups, skip):
     for group in range(groups):
         tile, b = (group + skip) // 8, (group + skip) % 8
         r, l = tiles(0, tile), tiles(1, tile)
-        if scale is not None:
-            r, l = r * scale[0], l * scale[1]
         dst[MAIN, 8 * group : 8 * group + 8] = halo_rows(r, l, b)
 
 
 def kernel(
     init_hbm, kap_hbm, guess_hbm, c_out, f_out,
-    ie, ke, ce, sp, si, pt, gs, got, us, ur, xs, xb, ph, phs, qh, qhs, ga, gb, oc, of, w0, w1, w2,
-    ld, st_s, st_r, co_s, co_r, row_s, row_r, a_s, a_r, h_s, h_r, e_s, e_r, sh_s, sh_r, eb_s, eb_r,
+    ie, ke, ce, sp, si, pt, gs, gx, got, gp, us, ur, xs, xb, ph, phs, qh, qhs, ga, gb, oc, of, w0, w1, w2,
+    ld, st_s, st_r, co_s, co_r, row_s, row_r, a_s, a_r, h_s, h_r, e_s, e_r, k_s, k_r, sh_s, sh_r, eb_s, eb_r,
     u_s, u_r, x_s, x_r, xe_s, xe_r, o_s, o_r,
 ):
     t, sx, sy = lax.axis_index("tm"), lax.axis_index("sx"), lax.axis_index("sy")
     nx, ny = lax.axis_size("sx"), lax.axis_size("sy")
     c, p = t // 2, lax.rem(t, 2)
     even, odd = p == 0, p == 1
-    up, down = lax.rem(sx + nx - 1, nx), lax.rem(sx + 1, nx)
-    left, right = lax.rem(sy + ny - 1, ny), lax.rem(sy + 1, ny)
+    up, down, left, right = sx - 1, sx + 1, sy - 1, sy + 1
+    has_up, has_down, has_left, has_right = sx > 0, sx < nx - 1, sy > 0, sy < ny - 1
+    tall, broad = has_up.astype(jnp.int32) + has_down, has_left.astype(jnp.int32) + has_right
     partner = t + 1 - 2 * p
     sends_guess = t <= 12
     work = (w0, w1, w2)
@@ -94,17 +92,42 @@
             cp.start()
 
     barrier = pltpu.get_barrier_semaphore()
-    got[...] = jnp.zeros(got.shape, F32)
+    for ref in (got, si, gs, gx):
+        ref[...] = jnp.zeros(ref.shape, F32)
+    for ref in (ie, ke, ce):
+        for rows in (slice(0, 16), slice(EXT - 16, EXT)):
+            ref[:, rows] = jnp.zeros((ref.shape[0], 16, 128), F32)
 
     def greet(d, carry):
         pl.semaphore_signal(barrier, inc=1, device_id={"tm": lax.rem(t + d, 2 * CHIPS)}, device_id_type=MESH)
         return carry
 
     lax.fori_loop(1, 2 * CHIPS, greet, 0)
-    near = [{"sx": up}, {"sx": down}, {"sy": left}, {"sy": right}]
-    near += [{"sx": v, "sy": h} for v in (up, down) for h in (left, right)]
-    for there in near:
-        pl.semaphore_signal(barrier, inc=1, device_id=there, device_id_type=MESH)
+    for v, has_v in ((0, True), (up, has_up), (down, has_down)):
+        for h, has_h in ((0, True), (left, has_left), (right, has_right)):
+            there = ({"sx": v} if has_v is not True else {}) | ({"sy": h} if has_h is not True else {})
+            if there:
+
+                @pl.when(has_v & has_h)
+                def _():
+                    pl.semaphore_signal(barrier, inc=1, device_id=there, device_id_type=MESH)
+
+
+    def greet_all(has, **there):
+        @pl.when(has)
+        def _():
+            def signal(i, carry):
+                pl.semaphore_signal(barrier, inc=1, device_id={"tm": 2 * i + p, **there}, device_id_type=MESH)
+                return carry
+
+            lax.fori_loop(0, CHIPS, signal, 0)
+
+    for h, has_h in ((left, has_left), (right, has_right)):
+        greet_all(has_h, sy=h)
+    for owner, v, has_v in ((0, up, has_up), (CHIPS - 1, down, has_down)):
+        greet_all((c == owner) & has_v, sx=v)
+        for h, has_h in ((left, has_left), (right, has_right)):
+            greet_all((c == owner) & has_v & has_h, sx=v, sy=h)
     for w in work:
         w[...] = jnp.zeros(w.shape, F32)
 
@@ -113,20 +136,30 @@
 
     def strip_copies(n, lo, hi):
         copies = []
-        for side, h in enumerate((left, right)):
+        for side, (h, sends, gets) in enumerate(((left, has_left, has_right), (right, has_right, has_left))):
             k = 2 * n + side
             f = pl.ds(lo, hi - lo)
-            copies.append(remote(sp.at[side, f], si.at[side, f, 1:5], st_s.at[k], st_r.at[k], {"sy": h}))
-            copies.append(remote(sp.at[side, f, 3], si.at[side, f, 0], co_s.at[2 * k], co_r.at[2 * k], {"sx": down, "sy": h}))
-            copies.append(remote(sp.at[side, f, 0], si.at[side, f, 5], co_s.at[2 * k + 1], co_r.at[2 * k + 1], {"sx": up, "sy": h}))
+            cp = remote(sp.at[side, f], si.at[side, f, 1:5], st_s.at[k], st_r.at[k], {"sy": h})
+            copies.append((cp, sends, gets))
+            cp = remote(sp.at[side, f, 3], si.at[side, f, 0], co_s.at[2 * k], co_r.at[2 * k], {"sx": down, "sy": h})
+            copies.append((cp, sends & has_down, gets & has_up))
+            cp = remote(sp.at[side, f, 0], si.at[side, f, 5], co_s.at[2 * k + 1], co_r.at[2 * k + 1], {"sx": up, "sy": h})
+            copies.append((cp, sends & has_up, gets & has_down))
         return copies
 
     def row_copies(n, ref):
         a, b, m = 2 * n, 2 * n + 1, pl.ds(0, MAIN)
-        return [
-            remote(ref.at[m, 16:32], ref.at[m, EXT - 16 : EXT], row_s.at[a], row_r.at[a], {"sx": up}),
-            remote(ref.at[m, EXT - 32 : EXT - 16], ref.at[m, 0:16], row_s.at[b], row_r.at[b], {"sx": down}),
-        ]
+        above = remote(ref.at[m, 16:32], ref.at[m, EXT - 16 : EXT], row_s.at[a], row_r.at[a], {"sx": up})
+        below = remote(ref.at[m, EXT - 32 : EXT - 16], ref.at[m, 0:16], row_s.at[b], row_r.at[b], {"sx": down})
+        return [(above, has_up, has_down), (below, has_down, has_up)]
+
+    def start_near(copies):
+        for cp, sends, _ in copies:
+            pl.when(sends)(cp.start)
+
+    def await_near(copies):
+        for cp, _, gets in copies:
+            pl.when(gets)(cp.wait_recv)
 
     def main_copy(i, slot):
         start = jnp.clip(32 * i - 8, 0, ROWS - BLOCK)
@@ -134,73 +167,89 @@
         dst = got.at[slot, :, pl.ds(pl.multiple_of(start + 16 - 32 * i, 8), BLOCK)]
         return remote(src, dst, a_s.at[i], a_r.at[slot], {"tm": 2 * i + p})
 
-    def side_copy(i, slot):
-        return remote(pt.at[i], gs.at[slot], h_s.at[i], h_r.at[slot], {"tm": 2 * i + p})
-
-    def top_copy(slot):
-        return remote(ce.at[:, 0:16], got.at[slot, :, 0:16], e_s.at[0], e_r.at[slot], {"tm": p})
-
-    def bottom_copy(slot):
-        return remote(ce.at[:, EXT - 16 : EXT], got.at[slot, :, 48:64], e_s.at[1], e_r.at[slot], {"tm": 2 * CHIPS - 2 + p})
+    def side_copy(side, i, slot):
+        there = {"tm": 2 * i + p, "sy": (left, right)[side]}
+        return remote(pt.at[side, i], gs.at[slot, side], h_s.at[side, i], h_r.at[slot, side], there)
+
+    def edge_copy(low, slot):
+        if low:
+            there = {"tm": p, "sx": down}
+            return remote(ce.at[:, EXT - 32 : EXT - 16], got.at[slot, :, 0:16], e_s.at[0], e_r.at[slot], there)
+        there = {"tm": 2 * CHIPS - 2 + p, "sx": up}
+        return remote(ce.at[:, 16:32], got.at[slot, :, 48:64], e_s.at[1], e_r.at[slot], there)
+
+    def corner_copy(low, side, slot):
+        there = {"tm": p, "sx": down} if low else {"tm": 2 * CHIPS - 2 + p, "sx": up}
+        there["sy"] = (left, right)[side]
+        src = pt.at[side, CHIPS if low else CHIPS + 1]
+        return remote(src, gx.at[slot, side], k_s.at[2 * low + side], k_r.at[slot, side], there)
+
+    def to_owners(act):
+        for side, has in enumerate((has_left, has_right)):
+
+            @pl.when(has)
+            def _():
+                def one(i, carry):
+                    act(side_copy(side, i, c))
+                    return carry
+
+                lax.fori_loop(0, CHIPS, one, 0)
+
+        for low, has in enumerate((has_up, has_down)):
+
+            @pl.when(has)
+            def _():
+                act(edge_copy(low, c))
+
+            for side, beside in enumerate((has_left, has_right)):
+
+                @pl.when(has & beside)
+                def _():
+                    act(corner_copy(low, side, c))
 
     guess_near = strip_copies(0, 2, 3) + row_copies(2, ce)
     other_near = strip_copies(1, 0, 2) + row_copies(1, ke) + row_copies(0, ie)
 
     def send_main(d, carry):
         main_copy(lax.rem(c + d, CHIPS), c).start()
-        return carry
-
-    def send_side(d, carry):
-        side_copy(lax.rem(c + d, CHIPS), c).start()
         return carry
 
     for cp in loads[2]:
         cp.wait()
     sp[0, 2] = pack(ce[0, 16 : 16 + ROWS], 0)
     sp[1, 2] = pack(ce[MAIN - 1, 16 : 16 + ROWS], 16)
-    pl.semaphore_wait(barrier, 2 * CHIPS - 1 + 8)
-    for cp in guess_near:
-        cp.start()
-
-    @pl.when(sends_guess)
-    def _():
-        lax.fori_loop(1, EARLY, send_main, 0)
-
+    lane = lax.broadcasted_iota(jnp.int32, (8, 128), 1)
+    none = jnp.zeros((8, 128), F32)
+    for side in range(2):
+        tiles = [none] + [sp[side, 2, k] for k in range(4)] + [none]
+        for i in range(CHIPS):
+            q, late = i // 2, i % 2
+            back, cut = (96, 96) if late else (32, 32)
+            a, b = pltpu.roll(tiles[q + late], back, 1), pltpu.roll(tiles[q + late + 1], back, 1)
+            pt[side, i] = jnp.where(lane < cut, a, b)
+        pt[side, CHIPS] = pltpu.roll(tiles[4], 32, 1)
+        pt[side, CHIPS + 1] = pltpu.roll(tiles[1], 96, 1)
     for n, ref in ((0, ie), (1, ke)):
         for cp in loads[n]:
             cp.wait()
         sp[0, n] = pack(ref[0, 16 : 16 + ROWS], 0)
         sp[1, n] = pack(ref[MAIN - 1, 16 : 16 + ROWS], 16)
-    for cp in other_near:
-        cp.start()
-
-    for cp in guess_near:
-        cp.wait_recv()
-    lane = lax.broadcasted_iota(jnp.int32, (8, 128), 1)
-    for i in range(CHIPS):
-        q, late = i // 2, i % 2
-        back, cut = (96, 96) if late else (32, 32)
-        for side in range(2):
-            a, b = si[side, 2, q + late], si[side, 2, q + late + 1]
-            pt[i, side] = jnp.where(lane < cut, pltpu.roll(a, back, 1), pltpu.roll(b, back, 1))
+    pl.semaphore_wait(barrier, 2 * CHIPS - 1 + tall + broad + tall * broad + CHIPS * broad + tall + tall * broad)
+
+    start_near(other_near + guess_near)
 
     @pl.when(sends_guess)
     def _():
-        lax.fori_loop(1, CHIPS, send_side, 0)
-
-        @pl.when(c != 0)
-        def _():
-            top_copy(c).start()
-
-        @pl.when(c != CHIPS - 1)
-        def _():
-            bottom_copy(c).start()
-
-        lax.fori_loop(EARLY, CHIPS, send_main, 0)
+        to_owners(lambda cp: cp.start())
+        lax.fori_loop(1, CHIPS, send_main, 0)
+
 
     at = pl.multiple_of(32 * c, 32)
-    got[c] = ce[:, pl.ds(at, WIN)]
-    gs[c] = pt[c]
+    start = jnp.clip(32 * c - 8, 0, ROWS - BLOCK)
+    into = pl.ds(pl.multiple_of(start + 16 - 32 * c, 8), BLOCK)
+    got[c, :, into] = ce[:, pl.ds(pl.multiple_of(start + 16, 8), BLOCK)]
+
+    await_near(guess_near)
 
     mine = pl.multiple_of(8 + 128 * p, 8)
 
@@ -226,37 +275,47 @@
         for cp in own_even:
             cp.start()
 
-    for cp in other_near:
-        cp.wait_recv()
-    keep = (jnp.where(sy == ny - 1, 0.0, 1.0).astype(F32), jnp.where(sy == 0, 0.0, 1.0).astype(F32))
-    unpack(ke, lambda side, k: si[side, 1, k], EXT // 8, 6, keep)
+    await_near(other_near)
+    unpack(ke, lambda side, k: si[side, 1, k], EXT // 8, 6)
     unpack(ie, lambda side, k: si[side, 0, k], EXT // 8, 6)
-
-    @pl.when(sx == 0)
-    def _():
-        ke[:, 0:16] = jnp.zeros((WIDE, 16, 128), F32)
-
-    @pl.when(sx == nx - 1)
-    def _():
-        ke[:, EXT - 16 : EXT] = jnp.zeros((WIDE, 16, 128), F32)
 
     def window(m):
         @pl.when(m != c)
         def _():
             main_copy(c, m).wait_recv()
-            side_copy(c, m).wait_recv()
-
-            @pl.when(c == 0)
-            def _():
-                top_copy(m).wait_recv()
-
-            @pl.when(c == CHIPS - 1)
-            def _():
-                bottom_copy(m).wait_recv()
-
-        r, l = gs[m, 0], gs[m, 1]
+
+        pl.when(has_right)(lambda: side_copy(0, c, m).wait_recv())
+        pl.when(has_left)(lambda: side_copy(1, c, m).wait_recv())
+        outside = ((c == 0) & has_up) | ((c == CHIPS - 1) & has_down)
+
+        @pl.when(outside)
+        def _():
+            edge_copy(1, m).wait_recv()
+
+        @pl.when(outside & has_right)
+        def _():
+            corner_copy(1, 0, m).wait_recv()
+
+        @pl.when(outside & has_left)
+        def _():
+            corner_copy(1, 1, m).wait_recv()
+
+        outer = ((c == 0) & (lane < 32)) | ((c == CHIPS - 1) & (lane >= 96))
+        r, l = (jnp.where(outer, gx[m, n], gs[m, n]) for n in range(2))
         side = jnp.concatenate([halo_rows(r, l, b) for b in range(8)], axis=0)
         return jnp.concatenate([got[m], side[None]], axis=0)
+
+    def arrivals(count, act):
+        def one(d, carry):
+            m = lax.rem(c + CHIPS - d, CHIPS)
+
+            @pl.when(m < count)
+            def _():
+                act(m)
+
+            return carry
+
+        lax.fori_loop(0, CHIPS, one, 0)
 
     def u_copy(m):
         return remote(us.at[m], ur.at[m + 1], u_s.at[m], u_r.at[m], {"tm": partner})
@@ -286,12 +345,11 @@
 
     @pl.when(odd)
     def _():
-        def point(m, carry):
+        def point(m):
             us[m] = parts(window(m), ke[:, pl.ds(at, WIN)], work, True)[1]
             u_copy(m).start()
-            return carry
-
-        lax.fori_loop(0, 6, point, 0)
+
+        arrivals(6, point)
 
     @pl.when(even)
     def _():
@@ -299,16 +357,18 @@
         ur[0] = parts(ie[:, pl.ds(at, WIN)], kap0, work, True)[1]
         xs[0] = ie[:, pl.ds(at, WIN)]
 
+        def ready(m):
+            gp[m] = parts(window(m), ke[:, pl.ds(at, WIN)], work, False)
+
+        arrivals(7, ready)
+
         def point(j, carry):
-            kap = ke[:, pl.ds(at, WIN)]
-            part = parts(window(j - 1), kap, work, False)
-
             @pl.when(j > 1)
             def _():
                 u_copy(jnp.maximum(j - 2, 0)).wait_recv()
 
             x = xs[j - 1]
-            xs[j] = x + 4.0 * lap(x, kap, w2) + (ur[j - 1] + part)
+            xs[j] = x + 4.0 * lap(x, ke[:, pl.ds(at, WIN)], w2) + (ur[j - 1] + gp[j - 1])
             for_x(j, lambda cp: cp.start())
 
             @pl.when((j == c) & (half == 0))
@@ -405,26 +465,17 @@
 
     lax.fori_loop(0, 4, finish, 0)
 
-    for cp in guess_near + other_near:
-        cp.wait_send()
+    for cp, sends, _ in guess_near + other_near:
+        pl.when(sends)(cp.wait_send)
 
     @pl.when(sends_guess)
     def _():
         def sent(d, carry):
-            i = lax.rem(c + d, CHIPS)
-            main_copy(i, c).wait_send()
-            side_copy(i, c).wait_send()
+            main_copy(lax.rem(c + d, CHIPS), c).wait_send()
             return carry
 
         lax.fori_loop(1, CHIPS, sent, 0)
-
-        @pl.when(c != 0)
-        def _():
-            top_copy(c).wait_send()
-
-        @pl.when(c != CHIPS - 1)
-        def _():
-            bottom_copy(c).wait_send()
+        to_owners(lambda cp: cp.wait_send())
 
     @pl.when(odd)
     def _():
@@ -474,13 +525,14 @@
             out_specs=(pl.BlockSpec(memory_space=pltpu.VMEM),) * 2,
             scratch_shapes=[
                 vmem(WIDE, EXT, 128), vmem(WIDE, EXT, 128), vmem(MAIN, EXT, 128),
-                vmem(2, 3, 4, 8, 128), vmem(2, 3, 6, 8, 128), vmem(CHIPS, 2, 8, 128), vmem(CHIPS, 2, 8, 128),
-                vmem(CHIPS, MAIN, WIN, 128), vmem(6, WIDE, WIN, 128), vmem(7, WIDE, WIN, 128), vmem(8, WIDE, WIN, 128),
+                vmem(2, 3, 4, 8, 128), vmem(2, 3, 6, 8, 128), vmem(2, CHIPS + 2, 8, 128),
+                vmem(CHIPS, 2, 8, 128), vmem(CHIPS, 2, 8, 128),
+                vmem(CHIPS, MAIN, WIN, 128), vmem(7, WIDE, WIN, 128), vmem(6, WIDE, WIN, 128), vmem(7, WIDE, WIN, 128), vmem(8, WIDE, WIN, 128),
                 vmem(WIDE, HALF, 128), vmem(WIDE, HALF, 128), vmem(2, 4, 8, 128), vmem(WIDE, HALF, 128), vmem(2, 4, 8, 128),
                 vmem(4, WIDE, BLOCK, 128), vmem(4, WIDE, BLOCK, 128), vmem(4, 32, COLS), vmem(4, 32, COLS),
                 vmem(WIDE, WIN + 16, 128), vmem(WIDE, WIN + 16, 128), vmem(WIDE, WIN + 16, 128),
                 dma(12), dma(4), dma(4), dma(8), dma(8), dma(6), dma(6),
-                dma(8), dma(8), dma(8), dma(8), dma(2), dma(8), dma(4), dma(2), dma(2), dma(2),
+                dma(8), dma(8), dma(2, 8), dma(8, 2), dma(2), dma(8), dma(4), dma(8, 2), dma(4), dma(2), dma(2), dma(2),
                 dma(6), dma(6), dma(8), dma(4), dma(8), dma(2), dma(8), dma(8),
             ],
             compiler_params=pltpu.CompilerParams(

time: 52.4 us -> 45.3 us (0.86)
  the two profiles are of different devices: /device:TPU:25 before, /device:TPU:217 now
where the time goes in v3:
time: 45.3 us; the launch traced here: 45.1 us
  Pallas kernels  41.8 us (92%)
  local copies, waits for them, and re-layouts  2.72 us (6%)
  between operations  0.65 us (1%)
    pallas_call x1, Pallas kernels, on_device(): pl.pallas_call(kernel, out_shape=(tile, tile), in_specs=[pl.BlockSpec(mem...  41.8 us
    unnamed x4, local copies, waits for them, and re-layouts  2.72 us

profile of v3, /device:TPU:217, one launch (start us, length us, event | category | flops | bytes accessed | tf_op | source)
XLA Modules:
  0.0 45.1 jit_solution(13499671239667979260)
XLA Ops:
  0.6 41.8 %shard_map.50 = (f32[1,256,512]{2,1,0:T(8,128)}, f32[1,256,512]{2,1,0:T(8,128)}) custom-call(f32[256,512]{1,0:T(8,128)} %init_hbm.1, f32[256,512]{1,0:T(8,128)} %kap_hbm.1, f32[1,256,512]{2,1,0:T(8,128)} %guess_hbm.1), custom_call_target="tpu_custom_call" | custom-call | tf_op jit(solution)/shard_map/pallas_call | solution.py:521
  42.4 0.0 copy-start
  42.4 1.9 %copy.7 = f32[1,256,512]{2,1,0:T(8,128)} copy(f32[1,256,512]{2,1,0:T(8,128)} %get-tuple-element.4) | data formatting | bytes 1048576
  44.3 0.0 copy-done
  44.4 0.8 %copy.8 = f32[1,256,512]{2,1,0:T(8,128)} copy(f32[1,256,512]{2,1,0:T(8,128)S(1)} %copy-done) | data formatting | bytes 1048576
Async XLA Ops:
  42.4 1.9 %copy-start = (f32[1,256,512]{2,1,0:T(8,128)S(1)}, f32[1,256,512]{2,1,0:T(8,128)}, u32[]{:S(2)}) copy-start(f32[1,256,512]{2,1,0:T(8,128)} %get-tuple-element.5) | copy-start | bytes 1572868

commit v4 on v3

--- a/solution.py
+++ b/solution.py
@@ -260,11 +260,6 @@
             remote(si.at[:, 2, pl.ds(2 * h, 4)], phs, sh_s.at[2 * h + 1], sh_r.at[1], to),
         ]
 
-    @pl.when(odd & (c < CHIPS - 1))
-    def _():
-        for cp in shift(0) + shift(1):
-            cp.start()
-
     own_even = [
         remote(ce.at[:, pl.ds(136, HALF)], qh.at[0:MAIN], eb_s.at[0], eb_r.at[0], {"tm": partner}),
         remote(si.at[:, 2, pl.ds(2, 4)], qhs, eb_s.at[1], eb_r.at[1], {"tm": partner}),
@@ -312,6 +307,11 @@
             @pl.when(m < count)
             def _():
                 act(m)
+
+            @pl.when(odd & (c < CHIPS - 1) & (d == 2))
+            def _():
+                for cp in shift(0) + shift(1):
+                    cp.start()
 
             return carry
 
@@ -509,6 +509,14 @@
     lax.fori_loop(0, 4, landed, 0)
 
 
+def store(c_ref, f_ref, c_hbm, f_hbm, sem):
+    copies = [pltpu.make_async_copy(src, dst, sem.at[n]) for n, (src, dst) in enumerate(((c_ref, c_hbm), (f_ref, f_hbm)))]
+    for cp in copies:
+        cp.start()
+    for cp in copies:
+        cp.wait()
+
+
 def solution(mesh):
     def dma(*shape):
         return pltpu.SemaphoreType.DMA(shape) if shape else pltpu.SemaphoreType.DMA
@@ -518,7 +526,7 @@
 
     def on_device(initial, kappa, guess):
         tile = jax.ShapeDtypeStruct((1, ROWS, COLS), F32)
-        return pl.pallas_call(
+        c, f = pl.pallas_call(
             kernel,
             out_shape=(tile, tile),
             in_specs=[pl.BlockSpec(memory_space=pltpu.HBM)] * 3,
@@ -536,9 +544,17 @@
                 dma(6), dma(6), dma(8), dma(4), dma(8), dma(2), dma(8), dma(8),
             ],
             compiler_params=pltpu.CompilerParams(
-                collective_id=0, has_side_effects=True, vmem_limit_bytes=67043328
+                collective_id=0, has_side_effects=True, vmem_limit_bytes=32 * 2**20
             ),
-        )(initial, kappa, guess)
+        )(*(pltpu.with_memory_space_constraint(x, pltpu.HBM) for x in (initial, kappa, guess)))
+        return pl.pallas_call(
+            store,
+            out_shape=(tile, tile),
+            in_specs=[pl.BlockSpec(memory_space=pltpu.VMEM)] * 2,
+            out_specs=(pl.BlockSpec(memory_space=pltpu.HBM),) * 2,
+            scratch_shapes=[dma(2)],
+            compiler_params=pltpu.CompilerParams(vmem_limit_bytes=16 * 2**20),
+        )(c, f)
 
     return jax.shard_map(
         on_device,

time: 45.3 us -> 42.5 us (0.938)
  local copies, waits for them, and re-layouts: 2.72 us -> 0 us
    unnamed x4 -> x0, local copies, waits for them, and re-layouts: 2.72 us -> none
    pallas_call x1, Pallas kernels: 41.8 us -> 40.7 us  [on_device(): pl.pallas_call(kernel, out_shape=(tile, tile), in_specs=[pl.BlockSpec(mem...]
    pallas_call x0 -> x1, Pallas kernels: none -> 0.99 us  [on_device(): pl.pallas_call(store, out_shape=(tile, tile), in_specs=[pl.BlockSpec(memo...]
where the time goes in v4:
time: 42.5 us; the launch traced here: 42.3 us
  Pallas kernels  41.7 us (98%)
  between operations  0.64 us (2%)
    pallas_call x1, Pallas kernels, on_device(): pl.pallas_call(kernel, out_shape=(tile, tile), in_specs=[pl.BlockSpec(mem...  40.7 us
    pallas_call x1, Pallas kernels, on_device(): pl.pallas_call(store, out_shape=(tile, tile), in_specs=[pl.BlockSpec(memo...  0.99 us

profile of v4, /device:TPU:217, one launch (start us, length us, event | category | flops | bytes accessed | tf_op | source)
XLA Modules:
  0.0 42.3 jit_solution(4188647699149564103)
XLA Ops:
  0.6 40.7 %shard_map.50 = (f32[1,256,512]{2,1,0:T(8,128)S(1)}, f32[1,256,512]{2,1,0:T(8,128)S(1)}) custom-call(f32[256,512]{1,0:T(8,128)} %init_hbm.1, f32[256,512]{1,0:T(8,128)} %kap_hbm.1, f32[1,256,512]{2,1,0:T(8,128)} %guess_hbm.1), custom_call_target="tpu_custom_call" | custom-call | tf_op jit(solution)/shard_map/pallas_call | solution.py:529
  41.3 1.0 %shard_map.51 = (f32[1,256,512]{2,1,0:T(8,128)}, f32[1,256,512]{2,1,0:T(8,128)}) custom-call(f32[1,256,512]{2,1,0:T(8,128)S(1)} %get-tuple-element.4.c_ref, f32[1,256,512]{2,1,0:T(8,128)S(1)} %get-tuple-element.5.f_ref), custom_call_target="tpu_custom_call" | custom-call | tf_op jit(solution)/shard_map/pallas_call | solution.py:550

commit v5 on v4

--- a/solution.py
+++ b/solution.py
@@ -147,10 +147,10 @@
             copies.append((cp, sends & has_up, gets & has_down))
         return copies
 
-    def row_copies(n, ref):
+    def row_copies(n, ref, deep=16):
         a, b, m = 2 * n, 2 * n + 1, pl.ds(0, MAIN)
-        above = remote(ref.at[m, 16:32], ref.at[m, EXT - 16 : EXT], row_s.at[a], row_r.at[a], {"sx": up})
-        below = remote(ref.at[m, EXT - 32 : EXT - 16], ref.at[m, 0:16], row_s.at[b], row_r.at[b], {"sx": down})
+        above = remote(ref.at[m, 16 : 16 + deep], ref.at[m, EXT - 16 : EXT - 16 + deep], row_s.at[a], row_r.at[a], {"sx": up})
+        below = remote(ref.at[m, EXT - 16 - deep : EXT - 16], ref.at[m, 16 - deep : 16], row_s.at[b], row_r.at[b], {"sx": down})
         return [(above, has_up, has_down), (below, has_down, has_up)]
 
     def start_near(copies):
@@ -207,8 +207,11 @@
                 def _():
                     act(corner_copy(low, side, c))
 
-    guess_near = strip_copies(0, 2, 3) + row_copies(2, ce)
-    other_near = strip_copies(1, 0, 2) + row_copies(1, ke) + row_copies(0, ie)
+    guess_near = strip_copies(0, 2, 3) + row_copies(2, ce, 8)
+    other_near = strip_copies(1, 1, 2) + row_copies(1, ke)
+    uses_initial = even | (c == 0)
+    for cp, sends, gets in strip_copies(2, 0, 1) + row_copies(0, ie):
+        other_near.append((cp, sends & uses_initial, gets & uses_initial))
 
     def send_main(d, carry):
         main_copy(lax.rem(c + d, CHIPS), c).start()
@@ -272,7 +275,10 @@
 
     await_near(other_near)
     unpack(ke, lambda side, k: si[side, 1, k], EXT // 8, 6)
-    unpack(ie, lambda side, k: si[side, 0, k], EXT // 8, 6)
+
+    @pl.when(uses_initial)
+    def _():
+        unpack(ie, lambda side, k: si[side, 0, k], EXT // 8, 6)
 
     def window(m):
         @pl.when(m != c)
@@ -539,7 +545,7 @@
                 vmem(WIDE, HALF, 128), vmem(WIDE, HALF, 128), vmem(2, 4, 8, 128), vmem(WIDE, HALF, 128), vmem(2, 4, 8, 128),
                 vmem(4, WIDE, BLOCK, 128), vmem(4, WIDE, BLOCK, 128), vmem(4, 32, COLS), vmem(4, 32, COLS),
                 vmem(WIDE, WIN + 16, 128), vmem(WIDE, WIN + 16, 128), vmem(WIDE, WIN + 16, 128),
-                dma(12), dma(4), dma(4), dma(8), dma(8), dma(6), dma(6),
+                dma(12), dma(6), dma(6), dma(12), dma(12), dma(6), dma(6),
                 dma(8), dma(8), dma(2, 8), dma(8, 2), dma(2), dma(8), dma(4), dma(8, 2), dma(4), dma(2), dma(2), dma(2),
                 dma(6), dma(6), dma(8), dma(4), dma(8), dma(2), dma(8), dma(8),
             ],

time: 42.5 us -> 41.7 us (0.981)
  Pallas kernels: 41.7 us -> 40.9 us
    pallas_call x1, Pallas kernels: 40.7 us -> 39.9 us  [on_device(): pl.pallas_call(kernel, out_shape=(tile, tile), in_specs=[pl.BlockSpec(mem...]
where the time goes in v5:
time: 41.7 us; the launch traced here: 41.6 us
  Pallas kernels  40.9 us (98%)
  between operations  0.64 us (2%)
    pallas_call x1, Pallas kernels, on_device(): pl.pallas_call(kernel, out_shape=(tile, tile), in_specs=[pl.BlockSpec(mem...  39.9 us
    pallas_call x1, Pallas kernels, on_device(): pl.pallas_call(store, out_shape=(tile, tile), in_specs=[pl.BlockSpec(memo...  0.99 us

profile of v5, /device:TPU:217, one launch (start us, length us, event | category | flops | bytes accessed | tf_op | source)
XLA Modules:
  0.0 41.6 jit_solution(9037978735203718045)
XLA Ops:
  0.6 39.9 %shard_map.50 = (f32[1,256,512]{2,1,0:T(8,128)S(1)}, f32[1,256,512]{2,1,0:T(8,128)S(1)}) custom-call(f32[256,512]{1,0:T(8,128)} %init_hbm.1, f32[256,512]{1,0:T(8,128)} %kap_hbm.1, f32[1,256,512]{2,1,0:T(8,128)} %guess_hbm.1), custom_call_target="tpu_custom_call" | custom-call | tf_op jit(solution)/shard_map/pallas_call | solution.py:535
  40.6 1.0 %shard_map.51 = (f32[1,256,512]{2,1,0:T(8,128)}, f32[1,256,512]{2,1,0:T(8,128)}) custom-call(f32[1,256,512]{2,1,0:T(8,128)S(1)} %get-tuple-element.4.c_ref, f32[1,256,512]{2,1,0:T(8,128)S(1)} %get-tuple-element.5.f_ref), custom_call_target="tpu_custom_call" | custom-call | tf_op jit(solution)/shard_map/pallas_call | solution.py:556

commit v6 on v5

--- a/solution.py
+++ b/solution.py
@@ -92,8 +92,10 @@
             cp.start()
 
     barrier = pltpu.get_barrier_semaphore()
-    for ref in (got, si, gs, gx):
+    for ref in (si, gs, gx):
         ref[...] = jnp.zeros(ref.shape, F32)
+    for rows in (slice(0, 16), slice(WIN - 16, WIN)):
+        got[:, :, rows] = jnp.zeros((CHIPS, MAIN, 16, 128), F32)
     for ref in (ie, ke, ce):
         for rows in (slice(0, 16), slice(EXT - 16, EXT)):
             ref[:, rows] = jnp.zeros((ref.shape[0], 16, 128), F32)
@@ -457,16 +459,18 @@
 
         @pl.when(even)
         def _():
+            put(oc.at[b], of.at[b], odd_c, odd_f)
+            out_copy(b, 0).start()
+            out_copy(b, 1).start()
             put(c_out.at[0, o], f_out.at[0, o], mid, even_f)
-            put(oc.at[b], of.at[b], odd_c, odd_f)
 
         @pl.when(odd)
         def _():
+            put(oc.at[b], of.at[b], mid, even_f)
+            out_copy(b, 0).start()
+            out_copy(b, 1).start()
             put(c_out.at[0, o], f_out.at[0, o], odd_c, odd_f)
-            put(oc.at[b], of.at[b], mid, even_f)
-
-        out_copy(b, 0).start()
-        out_copy(b, 1).start()
+
         return carry
 
     lax.fori_loop(0, 4, finish, 0)

time: 41.7 us -> 41.6 us (level)
  no operation moved by 1% of the time
where the time goes in v6:
time: 41.6 us; the launch traced here: 41.5 us
  Pallas kernels  40.8 us (98%)
  between operations  0.64 us (2%)
    pallas_call x1, Pallas kernels, on_device(): pl.pallas_call(kernel, out_shape=(tile, tile), in_specs=[pl.BlockSpec(mem...  39.8 us
    pallas_call x1, Pallas kernels, on_device(): pl.pallas_call(store, out_shape=(tile, tile), in_specs=[pl.BlockSpec(memo...  0.99 us

profile of v6, /device:TPU:217, one launch (start us, length us, event | category | flops | bytes accessed | tf_op | source)
XLA Modules:
  0.0 41.5 jit_solution(1095357697285348618)
XLA Ops:
  0.6 39.8 %shard_map.50 = (f32[1,256,512]{2,1,0:T(8,128)S(1)}, f32[1,256,512]{2,1,0:T(8,128)S(1)}) custom-call(f32[256,512]{1,0:T(8,128)} %init_hbm.1, f32[256,512]{1,0:T(8,128)} %kap_hbm.1, f32[1,256,512]{2,1,0:T(8,128)} %guess_hbm.1), custom_call_target="tpu_custom_call" | custom-call | tf_op jit(solution)/shard_map/pallas_call | solution.py:539
  40.5 1.0 %shard_map.51 = (f32[1,256,512]{2,1,0:T(8,128)}, f32[1,256,512]{2,1,0:T(8,128)}) custom-call(f32[1,256,512]{2,1,0:T(8,128)S(1)} %get-tuple-element.4.c_ref, f32[1,256,512]{2,1,0:T(8,128)S(1)} %get-tuple-element.5.f_ref), custom_call_target="tpu_custom_call" | custom-call | tf_op jit(solution)/shard_map/pallas_call | solution.py:560
